TPU v7x, 512 devices: a whole 4x8x8 slice. The times are simulated.
512 devices in a mesh: band: 64 (over z_lo, y, core), strip: 8 (over z_hi, x).
Axes of the slice: x: 4, y: 8, z: 8 (z_hi: 2, z_lo: 4; z = z_hi * 4 + z_lo), core: 2. Of those that a mesh axis runs over, the one named last changes fastest.
Arguments:
- activations: bfloat16 [64, 320, 48, 128], P('band', None, 'strip'), may hold values from -16 to 16
- out_grad: bfloat16 [64, 320, 48, 128], P('band', None, 'strip'), may hold values from -6 to 6
- kernel: bfloat16 [320, 9, 320], P('band', None, 'strip'), may hold values from -0.109375 to 0.109375
Outputs:
- input_grad: bfloat16 [64, 320, 48, 128], P('band', None, 'strip')
- kernel_grad: float32 [320, 9, 320], P('band', None, 'strip')
All inputs are finite; a program needn't handle non-finite values.
Results may differ from a plain program's by a relative error of at most 0.001.
Values may be sent and summed in bfloat16 or wider, within the bound.
A program may use at most 64 MiB of HBM per device.

v0:
```python
import math

import jax
import jax.numpy as jnp
from jax import lax
from jax.sharding import PartitionSpec as P

OFFSETS = ((-1, -1), (-1, 0), (-1, 1), (0, -1), (0, 0), (0, 1), (1, -1), (1, 0), (1, 1))


def extended(cells, sides, width):
    for axis, dim in sides:
        count = lax.axis_size(axis)
        ends = count - 1
        head = lax.slice_in_dim(cells, 0, width, axis=dim)
        tail = lax.slice_in_dim(cells, cells.shape[dim] - width, cells.shape[dim], axis=dim)
        cells = jnp.concatenate(
            [
                lax.ppermute(tail, axis, [(i, (i + 1) % count) for i in range(ends)]),
                cells,
                lax.ppermute(head, axis, [((i + 1) % count, i) for i in range(ends)]),
            ],
            axis=dim,
        )
    return cells


def tap_slice(field, row_step, col_step):
    row_count = field.shape[2] - 2
    col_count = field.shape[3] - 2
    return field[
        :, :, 1 + row_step : 1 + row_step + row_count, 1 + col_step : 1 + col_step + col_count
    ]


def body(activations, out_grad, kernel):
    images = activations.shape[0]
    row_count = activations.shape[2]
    col_count = activations.shape[3]
    cell_total = images * lax.axis_size("band") * row_count * lax.axis_size("strip") * col_count
    grad_scale = 1.0 / math.sqrt(cell_total)
    grad_padded = extended(out_grad, (("strip", 2),), 1)
    grad_padded = jnp.pad(grad_padded, ((0, 0), (0, 0), (0, 0), (1, 1)))
    kernel_full_cols = lax.all_gather(kernel, "strip", axis=2, tiled=True)
    kernel_whole = lax.all_gather(kernel_full_cols, "band", axis=0, tiled=True)
    summed = jnp.zeros((images, kernel_whole.shape[0], row_count, col_count), jnp.float32)
    for tap_index, (row_step, col_step) in enumerate(OFFSETS):
        shifted = tap_slice(grad_padded, -row_step, -col_step)
        summed = summed + jnp.einsum(
            "io,bohw->bihw",
            kernel_whole[:, tap_index, :],
            shifted,
            preferred_element_type=jnp.float32,
        )
    input_grad = summed.astype(jnp.bfloat16)
    blocks = []
    for tap_index, (row_step, col_step) in enumerate(OFFSETS):
        grad_side = tap_slice(grad_padded, -row_step, -col_step)
        blocks.append(
            jnp.einsum("bihw,bohw->io", activations, grad_side, preferred_element_type=jnp.float32)
        )
    partial_value = lax.psum_scatter(
        jnp.stack(blocks, axis=1), "band", scatter_dimension=0, tiled=True
    )
    kernel_sum = lax.psum_scatter(partial_value, "strip", scatter_dimension=2, tiled=True)
    return (input_grad, kernel_sum * grad_scale)


def solution(mesh):
    in_specs = (
        P("band", None, "strip", None),
        P("band", None, "strip", None),
        P("band", None, "strip"),
    )
    out_specs = (P("band", None, "strip", None), P("band", None, "strip"))
    return jax.shard_map(body, mesh=mesh, in_specs=in_specs, out_specs=out_specs, check_vma=False)
```

profile of v0, /device:TPU:1, one launch (start us, length us, event | category | flops | bytes accessed | tf_op | source)
XLA Modules:
  0.0 527.3 jit_solution(4342535424170789729)
XLA Ops:
  7.2 0.0 copy-start
  7.2 0.0 all-gather.2.cloned.1.call-start
  7.2 0.9 copy.21
  8.1 0.0 copy-start.1
  8.2 44.2 %all_gather.6 = bf16[5,9,320]{1,0,2:T(8,128)(2,1)S(1)} all-gather(bf16[5,9,40]{1,0,2:T(8,128)(2,1)S(1)} %copy.21), channel_id=1, replica_groups=mesh['band'=64,'strip'=8] {'strip'}, dimensions={2}, use_global_device_ids=true | all-gather | bytes 32400 | tf_op jit(solution)/shard_map/all_gather | solution.py:44
  52.3 1.0 copy.22
  53.3 0.0 all-gather.2.cloned.1.call-update
  53.3 0.0 reduce-scatter.3.cloned.1.call-start
  53.4 0.9 fusion.42
  54.3 1.3 collective-permute-start.1
  55.6 4.0 collective-permute-start
  59.6 0.1 collective-permute-done.1
  59.7 1.4 collective-permute-done
  61.1 1.7 fusion.6
  62.8 0.0 copy-done
  62.8 1.3 fusion.17
  64.1 0.0 copy-done.1
  64.1 1.3 fusion.16
  65.4 1.3 fusion.15
  66.6 1.3 fusion.14
  67.9 1.2 fusion.13
  69.1 1.3 fusion.12
  70.4 1.3 fusion.11
  71.6 1.2 fusion.10
  72.9 1.2 fusion.9
  74.1 9.0 %copy.33 = f32[320,9,320]{2,1,0:T(8,128)} copy(f32[320,9,320]{0,2,1:T(8,128)} %fusion.9) | data formatting | bytes 7372800 | tf_op jit(solution)/shard_map/stack | solution.py:63
  83.1 0.0 reduce-scatter.3.cloned.1.call-update
  83.1 1.3 dynamic-slice
  85.0 96.0 %all-gather.2.cloned.1.call-done = bf16[320,9,320]{2,1,0:T(8,128)(2,1)} async-done(((bf16[5,9,320]{2,1,0:T(8,128)(2,1)}), bf16[320,9,320]{2,1,0:T(8,128)(2,1)}) %all-gather.2.cloned.1.call-update) | async-done | bytes 1843216 | tf_op jit(solution)/shard_map/all_gather | solution.py:45
  181.0 10.5 %fusion.41 = (bf16[320,1,320]{2,1,0:T(2,128)(2,1)S(1)}, bf16[320,1,320]{2,1,0:T(2,128)(2,1)S(1)}, bf16[320,1,320]{2,1,0:T(2,128)(2,1)S(1)}, bf16[320,1,320]{2,1,...) fusion(bf16[320,9,320]{2,1,0:T(8,128)(2,1)} %all-gather.2.clone, ...), kind=kLoop, calls=%fused_computation.73 | loop fusion | bytes 3686400 | tf_op jit(solution)/shard_map/slice | solution.py:51
  191.5 0.4 fusion.32
  191.9 0.5 fusion.31
  192.4 0.4 convolution_add_fusion.6
  192.9 0.4 convolution_add_fusion.5
  193.3 0.5 convolution_add_fusion.4
  193.8 0.4 convolution_add_fusion.3
  194.2 0.4 convolution_add_fusion.2
  194.6 0.5 convolution_add_fusion.1
  195.1 1.2 fusion.8
  196.4 275.6 %reduce-scatter.3.cloned.1.call-done = f32[5,9,320]{2,1,0:T(8,128)} async-done(((f32[320,9,320]{2,1,0:T(8,128)}), f32[5,9,320]{2,1,0:T(8,128)}) %reduce-scatter.3.cloned.1.call-update) | async-done | bytes 57616 | tf_op jit(solution)/shard_map/reduce_scatter | solution.py:62
  471.9 47.8 %all-reduce.1 = f32[5,9,320]{2,1,0:T(8,128)S(1)} all-reduce(f32[5,9,320]{2,1,0:T(8,128)} %reduce-scatter.3.cloned.1.call-done), channel_id=3, replica_groups=mesh['band'=64,'strip'=8] {'strip'}, use_global_device_ids=true, to_apply=%region_1.2.clone | all-reduce | flops 14400 | bytes 115200
  519.7 0.1 dynamic-slice_multiply_fusion
  519.8 0.6 copy.34
Async XLA Ops:
  7.2 55.6 %copy-start = (bf16[1,320,6,128]{3,1,2,0:T(8,128)(2,1)S(1)}, bf16[1,320,6,128]{3,1,2,0:T(8,128)(2,1)}, u32[]{:S(2)}) copy-start(bf16[1,320,6,128]{3,1,2,0:T(8,128)(2,1)} %param.3) | copy-start | bytes 1474564
  7.2 173.8 %all-gather.2.cloned.1.call-start = ((), (), s32[]{:S(2)}) async-start(), calls=%async_computation.1 | async-start | bytes 3993600 | tf_op jit(solution)/shard_map/all_gather | solution.py:45
  8.1 55.9 %copy-start.1 = (bf16[1,320,6,128]{3,1,2,0:T(8,128)(2,1)S(1)}, bf16[1,320,6,128]{3,1,2,0:T(8,128)(2,1)}, u32[]{:S(2)}) copy-start(bf16[1,320,6,128]{3,1,2,0:T(8,128)(2,1)} %param.4) | copy-start | bytes 1474564
  53.3 418.6 %reduce-scatter.3.cloned.1.call-start = ((), (), s32[]{:S(2)}) async-start(), calls=%async_computation.2 | async-start | bytes 7987200 | tf_op jit(solution)/shard_map/reduce_scatter | solution.py:62
  54.3 5.4 %collective-permute-start.1 = (bf16[1,320,1,128]{3,1,2,0:T(8,128)(2,1)S(1)}, bf16[1,320,1,128]{3,1,2,0:T(8,128)(2,1)S(1)}, u32[]{:S(2)}, u32[]{:S(2)}) collective-permute-start(bf16[1,320,1,128]{3,1,2,0:T(8,128)(2,1)S(1)} %get-tuple-element.18), channel_id=1, source_target_pairs={{1,0},{2,1},{3,2},{4,3},{5,4},{6,5},{7,6},{9,8},{10,9},{11,10},{12... | collective-permute-start | bytes 245768 | tf_op jit(solution)/shard_map/ppermute | solution.py:21
  55.6 5.5 %collective-permute-start = (bf16[1,320,1,128]{3,1,2,0:T(8,128)(2,1)S(1)}, bf16[1,320,1,128]{3,1,2,0:T(8,128)(2,1)S(1)}, u32[]{:S(2)}, u32[]{:S(2)}) collective-permute-start(bf16[1,320,1,128]{3,1,2,0:T(8,128)(2,1)S(1)} %get-tuple-element.17), channel_id=1, source_target_pairs={{0,1},{1,2},{2,3},{3,4},{4,5},{5,6},{6,7},{8,9},{9,10},{10,11},{11... | collective-permute-start | bytes 245768 | tf_op jit(solution)/shard_map/ppermute | solution.py:19
Sparse Core Ops, SparseCore 0:
  53.5 127.4 all-gather.1
  183.8 288.0 reduce-scatter.2
where the time goes:
time: 533 us; the launch traced here: 527 us
  waiting for transfers between devices  373 us (70%)
  blocking collectives  91.9 us (17%)
  local copies, waits for them, and re-layouts  24.3 us (5%)
  matrix products  16.1 us (3%)
  between operations  14.8 us (3%)
  starting transfers between devices  5.36 us (1%)
    reduce_scatter x1, waiting for transfers between devices, body(): lax.psum_scatter(jnp.stack(blocks, axis=1), 'band', scatter_dimension=0,...  276 us
    all_gather x1, waiting for transfers between devices, body(): kernel_whole = lax.all_gather(kernel_full_cols, 'band', axis=0, tiled=True)  96 us
    unnamed x1, blocking collectives  47.8 us
    all_gather x1, blocking collectives, body(): kernel_full_cols = lax.all_gather(kernel, 'strip', axis=2, tiled=True)  44.2 us
    dot_general x9, matrix products, body(): jnp.einsum('bihw,bohw->io', activations, grad_side, preferred_element_typ...  11.3 us
  transfers between devices with their start and end apart: 4, of which 4 were waited for; matrix products, arithmetic and copies ran while one was open for 7% of the time, Pallas kernels for 0%

commit v1 on v0

v1 whole, which is shorter than its diff:
```python
import math

import jax
import jax.numpy as jnp
import numpy as np
from jax import lax
from jax.experimental import pallas as pl
from jax.experimental.pallas import tpu as pltpu
from jax.sharding import PartitionSpec as P

MESH = pl.DeviceIdType.MESH
BF16 = jnp.bfloat16
F32 = jnp.float32

ROWS = 6
CH = 320
WIDTH = 128
NX, NY, NZ = 4, 8, 8
ZL = 4
KI = 5
KO = 40
HALF = CH // 2
NT = (((1,), (1,)), ((), ()))


def permutation():
    perm = np.zeros((CH, CH), np.float32)
    for core in range(2):
        for m in range(HALF):
            perm[core * HALF + m, 2 * KI * (m // KI) + KI * core + m % KI] = 1.0
    return perm


def spread():
    out = np.zeros((3 * HALF, 32 * 16), np.float32)
    for j in range(3):
        for m in range(HALF):
            out[j * HALF + m, 16 * (m // KI) + j * KI + m % KI] = 1.0
    return out


def fdot(a, b, dims=(((1,), (0,)), ((), ()))):
    return lax.dot_general(a, b, dims, preferred_element_type=F32)


def kernel(
    scale, act_hbm, grad_hbm, piece_ref, perm_hbm, permt_hbm, spread_hbm,
    ig_ref, kg_ref,
    act, gext, perm, permt, spr, amat, q, p, wp, wmat, igs, igr,
    rx1, rz1, s1a, s1b, rx2, rz2, s2, s2r, ry,
    lsem, psem, prec, hsem, hrec, fsem, frec, gsem, grec, xsem, xrec, zsem, zrec, x2sem, x2rec, z2sem, z2rec, ysem, yrec, isem, irec,
):
    band = lax.axis_index("band")
    strip = lax.axis_index("strip")
    core = lax.rem(band, 2)
    y = lax.rem(band // 2, NY)
    zl = band // (2 * NY)
    x = lax.rem(strip, NX)
    zh = strip // NX
    z = zh * ZL + zl

    def at(zz, yy, xx):
        zzh, zzl = zz // ZL, lax.rem(zz, ZL)
        return ((zzl * NY + yy) * 2 + core, zzh * NX + xx)

    pair = (band + 1 - 2 * core, strip)
    down = (band, lax.rem(strip + 1, 8))
    up = (band, lax.rem(strip + 7, 8))
    xs = [lax.rem(x + d, NX) for d in range(1, NX)]
    ys = [lax.rem(y + d, NY) for d in range(1, NY)]
    zs = [lax.rem(z + d, NZ) for d in range(1, NZ)]
    xdev = [at(z, y, v) for v in xs]
    ydev = [at(z, v, x) for v in ys]
    zdev = [at(v, y, x) for v in zs]

    barrier = pltpu.get_barrier_semaphore()
    partners = [pair, down, up] + xdev + ydev + zdev
    for dev in partners:
        pl.semaphore_signal(barrier, inc=1, device_id=dev, device_id_type=MESH)

    local = [
        pltpu.make_async_copy(act_hbm, act.at[0], lsem.at[0]),
        pltpu.make_async_copy(grad_hbm, gext.at[0, pl.ds(1, ROWS)], lsem.at[1]),
        pltpu.make_async_copy(perm_hbm, perm, lsem.at[2]),
        pltpu.make_async_copy(permt_hbm, permt, lsem.at[3]),
        pltpu.make_async_copy(spread_hbm, spr, lsem.at[4]),
        pltpu.make_async_copy(piece_ref, wp.at[zh, x, zl, y], lsem.at[5]),
    ]
    for c in local:
        c.start()
    s2r[...] = jnp.zeros_like(s2r)

    def remote(src, dst, ss, rs, dev):
        c = pltpu.make_async_remote_copy(
            src_ref=src, dst_ref=dst, send_sem=ss, recv_sem=rs, device_id=dev, device_id_type=MESH
        )
        c.start()
        return c

    pl.semaphore_wait(barrier, len(partners))
    sent = []
    halo = [
        remote(grad_hbm.at[ROWS - 1], gext.at[0, 0], hsem.at[0], hrec.at[0], down),
        remote(grad_hbm.at[0], gext.at[0, ROWS + 1], hsem.at[1], hrec.at[1], up),
    ]
    swap = [
        remote(grad_hbm, gext.at[1, pl.ds(1, ROWS)], psem.at[0], prec.at[0], pair),
        remote(act_hbm, act.at[1], psem.at[1], prec.at[1], pair),
    ]
    local[5].wait()
    gx = [
        remote(piece_ref, wp.at[zh, x, zl, y], gsem.at[i], grec.at[i], xdev[i])
        for i in range(NX - 1)
    ]
    sent += halo + swap + gx

    lane = lax.broadcasted_iota(jnp.int32, (80, WIDTH), 1)
    zero8 = jnp.zeros((8, WIDTH), F32)

    def fill(img, e, keep=None):
        col = pl.ds(pl.multiple_of((img * 8 + e) * WIDTH, WIDTH), WIDTH)
        for pr in range(4):
            g = gext[img, e, 80 * pr : 80 * pr + 80, :].astype(F32)
            if keep is not None:
                g = jnp.where(keep, g, 0.0)
            nxt = jnp.where(lane == WIDTH - 1, 0.0, pltpu.roll(g, WIDTH - 1, 1))
            prv = jnp.where(lane == 0, 0.0, pltpu.roll(g, 1, 1))
            for h in range(2):
                sl = slice(40 * h, 40 * h + 40)
                block = jnp.concatenate([nxt[sl], g[sl], prv[sl], zero8], axis=0)
                base = (2 * pr + h) * 128
                q[base : base + 128, col] = block.astype(BF16)

    def fill_image(img):
        @pl.loop(1, ROWS + 1)
        def _(e):
            fill(img, e)

    def rows_image(img):
        mine = perm[pl.ds(pl.multiple_of(core * HALF, HALF), HALF), :]
        for h in range(0, ROWS, 2):
            pairh = jnp.concatenate([act[img, h], act[img, h + 1]], axis=1)
            base = img * ROWS * WIDTH + h * WIDTH
            amat[:, base : base + 2 * WIDTH] = fdot(mine, pairh).astype(BF16)

    local[1].wait()
    fill_image(0)
    local[0].wait()
    local[2].wait()
    rows_image(0)
    swap[0].wait_recv()
    fill_image(1)
    swap[1].wait_recv()
    rows_image(1)

    for c in gx:
        c.wait_recv()
    gz = [
        remote(wp.at[zh, :, zl, y], wp.at[zh, :, zl, y], gsem.at[3 + i], grec.at[3 + i], zdev[i])
        for i in range(NZ - 1)
    ]
    sent += gz

    span = ROWS * WIDTH

    def partial(j):
        @pl.loop(0, 4)
        def _(n):
            rows = pl.ds(pl.multiple_of(n * 256, 256), 256)
            total = fdot(amat[:, 0:span], q[rows, (2 - j) * WIDTH : (2 - j) * WIDTH + span], NT)
            total = total + fdot(
                amat[:, span : 2 * span], q[rows, (10 - j) * WIDTH : (10 - j) * WIDTH + span], NT
            )
            for h in range(2):
                sidx = 2 * n + h
                p[j, sidx // NX, lax.rem(sidx, NX)] = total[:, 128 * h : 128 * h + 128].reshape(
                    ZL, HALF // ZL, 128
                )

    def send_x(j):
        return [
            remote(p.at[j, :, xs[i]], rx1.at[j - 1, i], xsem.at[j - 1, i], xrec.at[j - 1, i], xdev[i])
            for i in range(NX - 1)
        ]

    partial(1)
    x1 = {1: send_x(1)}

    for c in halo:
        c.wait_recv()
    forward = [
        remote(gext.at[0, e], gext.at[1, e], fsem.at[i], frec.at[i], pair)
        for i, e in enumerate((0, ROWS + 1))
    ]
    sent += forward
    top, bottom = strip > 0, strip < 7
    fill(0, 0, top)
    fill(0, ROWS + 1, bottom)
    forward[0].wait_recv()
    fill(1, 0, top)
    forward[1].wait_recv()
    fill(1, ROWS + 1, bottom)

    partial(0)
    z1 = [
        remote(
            p.at[0, zs[i] // ZL, :, lax.rem(zs[i], ZL)], rz1.at[i], zsem.at[i], zrec.at[i], zdev[i]
        )
        for i in range(NZ - 1)
    ]
    partial(2)
    x1[2] = send_x(2)
    sent += x1[1] + z1 + x1[2]

    for c in gz:
        c.wait_recv()
    gy = [
        remote(wp.at[:, :, :, y], wp.at[:, :, :, y], gsem.at[10 + i], grec.at[10 + i], ydev[i])
        for i in range(NY - 1)
    ]
    sent += gy

    z2 = {}

    def second(j):
        for c in x1[j]:
            c.wait_recv()
        for h in range(2):
            total = p[j, h, x]
            for i in range(NX - 1):
                total = total + rx1[j - 1, i, h]
            s1a[j - 1, h] = total
        z2[j] = [
            remote(
                s1a.at[j - 1, zs[i] // ZL, lax.rem(zs[i], ZL)],
                rz2.at[j - 1, i], z2sem.at[j - 1, i], z2rec.at[j - 1, i], zdev[i],
            )
            for i in range(NZ - 1)
        ]

    second(1)
    for c in z1:
        c.wait_recv()
    total = p[0, zh, :, zl]
    for i in range(NZ - 1):
        total = total + rz1[i]
    s1b[...] = total
    x2 = [
        remote(s1b.at[xs[i]], rx2.at[i], x2sem.at[i], x2rec.at[i], xdev[i]) for i in range(NX - 1)
    ]
    second(2)
    sent += x2 + z2[1] + z2[2]

    for j in (1, 2):
        for c in z2[j]:
            c.wait_recv()
        total = s1a[j - 1, zh, zl]
        for i in range(NZ - 1):
            total = total + rz2[j - 1, i]
        s2[j] = total
    for c in x2:
        c.wait_recv()
    total = s1b[x]
    for i in range(NX - 1):
        total = total + rx2[i]
    s2[0] = total
    for j in range(3):
        for v in range(NY):
            s2r[v, j, 0:KI, :] = s2[j, KI * v : KI * v + KI, :]
    y3 = [
        remote(s2r.at[ys[i]], ry.at[i], ysem.at[i], yrec.at[i], ydev[i]) for i in range(NY - 1)
    ]
    sent += y3

    for c in gy:
        c.wait_recv()
    local[4].wait()
    for pr in range(4):
        both = jnp.concatenate(
            [wp[(2 * pr + h) // NX, (2 * pr + h) % NX].reshape(512, 128) for h in range(2)], axis=1
        )
        wmat[:, 256 * pr : 256 * pr + 256] = fdot(spr[...], both).astype(BF16)

    def image(img, put):
        for h in range(0, ROWS, 2):
            total = None
            for j in range(3):
                base = (img * 8 + h + 2 - j) * WIDTH
                term = fdot(wmat[HALF * j : HALF * j + HALF, :], q[:, base : base + 256])
                total = term if total is None else total + term
            total = total.astype(BF16)
            put(h, total[:, :WIDTH])
            put(h + 1, total[:, WIDTH:])

    def put_peer(h, v):
        igs[h] = v

    def put_own(h, v):
        igr[h, pl.ds(pl.multiple_of(core * HALF, HALF), HALF), :] = v

    image(1, put_peer)
    half = pl.ds(pl.multiple_of(core * HALF, HALF), HALF)
    back = remote(igs, igr.at[:, half], isem, irec, pair)
    sent.append(back)
    image(0, put_own)
    local[3].wait()
    back.wait_recv()
    for h in range(0, ROWS, 2):
        both = jnp.concatenate([igr[h], igr[h + 1]], axis=1)
        out = fdot(permt[...], both).astype(BF16)
        ig_ref[h] = out[:, :WIDTH]
        ig_ref[h + 1] = out[:, WIDTH:]

    for c in y3:
        c.wait_recv()
    total = s2r[y]
    for i in range(NY - 1):
        total = total + ry[i]
    kg_ref[...] = total * scale
    for c in sent:
        c.wait_send()


def body(activations, out_grad, weights):
    cells = 64 * 48 * 128
    scale = 1.0 / math.sqrt(cells)
    act = jnp.transpose(activations[0], (1, 0, 2))
    grad = jnp.transpose(out_grad[0], (1, 0, 2))
    piece = jnp.transpose(weights.reshape(KI, 3, 3, KO), (1, 0, 2, 3)).reshape(3 * KI, 3 * KO)
    piece = jnp.pad(piece, ((0, 1), (0, 8)))
    perm = permutation()
    hbm = pl.BlockSpec(memory_space=pl.ANY)
    vmem = pl.BlockSpec(memory_space=pltpu.VMEM)
    V = pltpu.VMEM
    D = pltpu.SemaphoreType.DMA

    def run(*args):
        kernel(scale, *args)

    ig, kg = pl.pallas_call(
        run,
        out_shape=(
            jax.ShapeDtypeStruct((ROWS, CH, WIDTH), BF16),
            jax.ShapeDtypeStruct((3, 8, 128), F32),
        ),
        in_specs=[hbm, hbm, vmem, hbm, hbm, hbm],
        out_specs=(vmem, vmem),
        scratch_shapes=[
            V((2, ROWS, CH, WIDTH), BF16),
            V((2, 8, CH, WIDTH), BF16),
            V((CH, CH), BF16),
            V((CH, CH), BF16),
            V((3 * HALF, 512), BF16),
            V((HALF, 2 * ROWS * WIDTH), BF16),
            V((1024, 2048), BF16),
            V((3, 2, NX, ZL, 40, 128), F32),
            V((2, NX, ZL, NY, 16, 128), BF16),
            V((3 * HALF, 1024), BF16),
            V((ROWS, HALF, WIDTH), BF16),
            V((ROWS, CH, WIDTH), BF16),
            V((2, NX - 1, 2, ZL, 40, 128), F32),
            V((NZ - 1, NX, 40, 128), F32),
            V((2, 2, ZL, 40, 128), F32),
            V((NX, 40, 128), F32),
            V((NX - 1, 40, 128), F32),
            V((2, NZ - 1, 40, 128), F32),
            V((3, 40, 128), F32),
            V((NY, 3, 8, 128), F32),
            V((NY - 1, 3, 8, 128), F32),
            D((6,)), D((2,)), D((2,)), D((2,)), D((2,)), D((2,)), D((2,)), D((17,)), D((17,)),
            D((2, 3)), D((2, 3)), D((7,)), D((7,)), D((3,)), D((3,)), D((2, 7)), D((2, 7)),
            D((7,)), D((7,)), D(()), D(()),
        ],
        compiler_params=pltpu.CompilerParams(
            collective_id=0, has_side_effects=True, vmem_limit_bytes=48 << 20
        ),
    )(
        act, grad, piece,
        jnp.asarray(perm, BF16), jnp.asarray(perm.T, BF16), jnp.asarray(spread(), BF16),
    )
    input_grad = jnp.transpose(ig, (1, 0, 2))[None]
    kg = kg[:, :KI, : 3 * KO].reshape(3, KI, 3, KO)
    kernel_grad = jnp.transpose(kg, (1, 0, 2, 3)).reshape(KI, 9, KO)
    return input_grad, kernel_grad


def solution(mesh):
    in_specs = (
        P("band", None, "strip", None),
        P("band", None, "strip", None),
        P("band", None, "strip"),
    )
    out_specs = (P("band", None, "strip", None), P("band", None, "strip"))
    return jax.shard_map(body, mesh=mesh, in_specs=in_specs, out_specs=out_specs, check_vma=False)
```

time: 533 us -> 66.3 us (0.12)
  waiting for transfers between devices: 373 us -> 0 us
  blocking collectives: 91.9 us -> 0 us
  Pallas kernels: 0 us -> 57.9 us
  local copies, waits for them, and re-layouts: 24.3 us -> 7.3 us
  matrix products: 16.1 us -> 0 us
  between operations: 14.8 us -> 0.66 us
  starting transfers between devices: 5.36 us -> 0 us
    reduce_scatter x1 -> x0, waiting for transfers between devices: 276 us -> none  [body(): lax.psum_scatter(jnp.stack(blocks, axis=1), 'band', scatter_dimension=0,...]
    all_gather x1 -> x0, waiting for transfers between devices: 96 us -> none  [body(): kernel_whole = lax.all_gather(kernel_full_cols, 'band', axis=0, tiled=True)]
    pallas_call x0 -> x1, Pallas kernels: none -> 57.9 us  [body(): pl.pallas_call(run, out_shape=(jax.ShapeDtypeStruct((ROWS, CH, WIDTH), BF...]
    unnamed x1 -> x0, blocking collectives: 47.8 us -> none
    all_gather x1 -> x0, blocking collectives: 44.2 us -> none  [body(): kernel_full_cols = lax.all_gather(kernel, 'strip', axis=2, tiled=True)]
    dot_general x18 -> x0, matrix products: 16.1 us -> none  [the longest x9 11.3 us: body(): jnp.einsum('bihw,bohw->io', activations, grad_side, preferred_element_typ...]
    slice x2 -> x1, local copies, waits for them, and re-layouts: 11.5 us -> 0.01 us  [body(): kg = kg[:, :KI, :3 * KO].reshape(3, KI, 3, KO)]
    another operation x1 -> x0, local copies, waits for them, and re-layouts: 8.98 us -> none  [body(): jnp.stack(blocks, axis=1)]
  transfers between devices with their start and end apart: 4 -> 0, of which waited for: 4 -> 0; matrix products, arithmetic and copies ran while one was open for 7% -> 0% of each run, Pallas kernels for 0% -> 0%
where the time goes in v1:
time: 66.3 us; the launch traced here: 65.9 us
  Pallas kernels  57.9 us (87%)
  local copies, waits for them, and re-layouts  7.3 us (11%)
    pallas_call x1, Pallas kernels, body(): pl.pallas_call(run, out_shape=(jax.ShapeDtypeStruct((ROWS, CH, WIDTH), BF...  57.9 us
    unnamed x11, local copies, waits for them, and re-layouts  5.75 us

profile of v1, /device:TPU:1, one launch (start us, length us, event | category | flops | bytes accessed | tf_op | source)
XLA Modules:
  0.0 65.9 jit_solution(14230773219309708038)
XLA Ops:
  0.6 0.7 %copy.17 = bf16[5,3,3,40]{3,2,0,1:T(4,128)(2,1)S(1)} copy(bf16[5,3,3,40]{3,0,2,1:T(8,128)(2,1)} %bitcast.25) | data formatting | bytes 7200 | tf_op jit(solution)/shard_map/reshape | solution.py:329
  1.4 0.1 reshape.17
  1.5 0.0 copy-start
  1.5 1.0 %copy-done = bf16[1,320,6,128]{3,1,2,0:T(8,128)(2,1)S(1)} copy-done((bf16[1,320,6,128]{3,1,2,0:T(8,128)(2,1)S(1)}, bf16[1,320,6,128]{3,1,2,0:T(8,128)(2,1)}, u32[]{:S(2)}) %copy-start) | copy-done | bytes 491544
  2.5 0.0 copy-start.1
  2.5 1.0 %copy-done.1 = bf16[1,320,6,128]{3,1,2,0:T(8,128)(2,1)S(1)} copy-done((bf16[1,320,6,128]{3,1,2,0:T(8,128)(2,1)S(1)}, bf16[1,320,6,128]{3,1,2,0:T(8,128)(2,1)}, u32[]{:S(2)}) %copy-start.1) | copy-done | bytes 491544
  3.5 0.0 copy-start.2
  3.5 1.0 %copy-done.2 = bf16[480,512]{1,0:T(8,128)(2,1)S(1)} copy-done((bf16[480,512]{1,0:T(8,128)(2,1)S(1)}, bf16[480,512]{1,0:T(8,128)(2,1)}, u32[]{:S(2)}) %copy-start.2) | copy-done | bytes 491544
  4.6 0.0 copy-start.3
  4.6 0.9 %copy-done.3 = bf16[320,320]{1,0:T(8,128)(2,1)S(1)} copy-done((bf16[320,320]{1,0:T(8,128)(2,1)S(1)}, bf16[320,320]{1,0:T(8,128)(2,1)}, u32[]{:S(2)}) %copy-start.3) | copy-done | bytes 204824
  5.5 0.0 copy-start.4
  5.5 0.9 %copy-done.4 = bf16[320,320]{1,0:T(8,128)(2,1)S(1)} copy-done((bf16[320,320]{1,0:T(8,128)(2,1)S(1)}, bf16[320,320]{1,0:T(8,128)(2,1)}, u32[]{:S(2)}) %copy-start.4) | copy-done | bytes 204824
  6.4 57.9 %shard_map.77 = (bf16[6,320,128]{2,1,0:T(8,128)(2,1)S(1)}, f32[3,8,128]{2,1,0:T(8,128)S(1)}) custom-call(bf16[6,320,128]{2,1,0:T(8,128)(2,1)S(1)} %bitcast.19, bf16[6,320,128]{2,1,0:T(8,128)(2,1)S(1)} %bitcast.20, bf16[16,128]{1,0:T(8,128)(2,1)S(1)} %pad.4.args_2_, bf16[320,320]{1,0:T(8,128)(2,1)S(1)} %copy-done.4, bf16[320,320]{1,0:T(8,128)(2,1)S(1)} %copy-done.3, ...), custom_call_target="tpu_custom_call" | custom-call | tf_op jit(solution)/shard_map/pallas_call | solution.py:340
  64.4 0.1 reshape.18
  64.5 0.6 copy.15
  65.1 0.8 %copy.19 = bf16[1,320,6,128]{3,1,2,0:T(8,128)(2,1)} copy(bf16[1,320,6,128]{3,1,2,0:T(8,128)(2,1)S(1)} %bitcast.18) | data formatting | bytes 983040
  (2 shorter events, 0.0 us)
Async XLA Ops:
  1.5 1.0 %copy-start = (bf16[1,320,6,128]{3,1,2,0:T(8,128)(2,1)S(1)}, bf16[1,320,6,128]{3,1,2,0:T(8,128)(2,1)}, u32[]{:S(2)}) copy-start(bf16[1,320,6,128]{3,1,2,0:T(8,128)(2,1)} %param.6) | copy-start | bytes 1474564
  2.5 1.0 %copy-start.1 = (bf16[1,320,6,128]{3,1,2,0:T(8,128)(2,1)S(1)}, bf16[1,320,6,128]{3,1,2,0:T(8,128)(2,1)}, u32[]{:S(2)}) copy-start(bf16[1,320,6,128]{3,1,2,0:T(8,128)(2,1)} %param.7) | copy-start | bytes 1474564
  3.5 1.0 %copy-start.2 = (bf16[480,512]{1,0:T(8,128)(2,1)S(1)}, bf16[480,512]{1,0:T(8,128)(2,1)}, u32[]{:S(2)}) copy-start(bf16[480,512]{1,0:T(8,128)(2,1)} %constant.11.clone.args_5_) | copy-start | bytes 1474564
  4.6 0.9 %copy-start.3 = (bf16[320,320]{1,0:T(8,128)(2,1)S(1)}, bf16[320,320]{1,0:T(8,128)(2,1)}, u32[]{:S(2)}) copy-start(bf16[320,320]{1,0:T(8,128)(2,1)} %constant.10.clone.args_4_) | copy-start | bytes 614404
  5.5 0.9 %copy-start.4 = (bf16[320,320]{1,0:T(8,128)(2,1)S(1)}, bf16[320,320]{1,0:T(8,128)(2,1)}, u32[]{:S(2)}) copy-start(bf16[320,320]{1,0:T(8,128)(2,1)} %constant.9.clone.args_3_) | copy-start | bytes 614404

commit v2 on v1

v2 whole, which is shorter than its diff:
```python
import math

import jax
import jax.numpy as jnp
import numpy as np
from jax import lax
from jax.experimental import pallas as pl
from jax.experimental.pallas import tpu as pltpu
from jax.sharding import PartitionSpec as P

MESH = pl.DeviceIdType.MESH
BF16 = jnp.bfloat16
F32 = jnp.float32

ROWS = 6
CH = 320
WIDTH = 128
NX, NY, NZ = 4, 8, 8
ZL = 4
KI = 5
KO = 40
HALF = CH // 2
NT = (((1,), (1,)), ((), ()))


def permutation():
    perm = np.zeros((CH, CH), np.float32)
    gather = np.zeros((2, 352, CH), np.float32)
    for core in range(2):
        for m in range(HALF):
            zy, k = m // KI, m % KI
            i = 2 * KI * zy + KI * core + k
            perm[i, core * HALF + m] = 1.0
            gather[core, m, i] = 1.0
            gather[core, HALF + 24 * (zy % NY) + KI * (zy // NY) + k, i] = 1.0
    return gather, perm


def spread():
    out = np.zeros((3 * HALF, 32 * 16), np.float32)
    for j in range(3):
        for m in range(HALF):
            out[j * HALF + m, 16 * (m // KI) + j * KI + m % KI] = 1.0
    return out


def fdot(a, b, dims=(((1,), (0,)), ((), ()))):
    return lax.dot_general(a, b, dims, preferred_element_type=F32)


def kernel(
    scale, act_hbm, grad_hbm, piece_ref, gather_hbm, permt_hbm, spread_hbm,
    ig_ref, kg_ref,
    act, gext, gather, permt, spr, amat, q, p, p2, wp, wmat, igs, igr,
    rx1, rz1, ry1, s1a, s1b, s1c, rx2, rx3, rz2, s2, s2r, ry, t2, t2r, rz3,
    lsem, psem, prec, hsem, hrec, fsem, frec, gsem, grec, xsem, xrec, zsem, zrec, rsem, rrec,
    x2sem, x2rec, x3sem, x3rec, z2sem, z2rec, ysem, yrec, z3sem, z3rec, isem, irec,
):
    band = lax.axis_index("band")
    strip = lax.axis_index("strip")
    core = lax.rem(band, 2)
    y = lax.rem(band // 2, NY)
    zl = band // (2 * NY)
    x = lax.rem(strip, NX)
    zh = strip // NX
    z = zh * ZL + zl

    def at(zz, yy, xx):
        zzh, zzl = zz // ZL, lax.rem(zz, ZL)
        return ((zzl * NY + yy) * 2 + core, zzh * NX + xx)

    pair = (band + 1 - 2 * core, strip)
    down = (band, lax.rem(strip + 1, 8))
    up = (band, lax.rem(strip + 7, 8))
    xs = [lax.rem(x + d, NX) for d in range(1, NX)]
    ys = [lax.rem(y + d, NY) for d in range(1, NY)]
    zs = [lax.rem(z + d, NZ) for d in range(1, NZ)]
    xdev = [at(z, y, v) for v in xs]
    ydev = [at(z, v, x) for v in ys]
    zdev = [at(v, y, x) for v in zs]

    barrier = pltpu.get_barrier_semaphore()
    partners = [pair, down, up] + xdev + ydev + zdev
    for dev in partners:
        pl.semaphore_signal(barrier, inc=1, device_id=dev, device_id_type=MESH)

    local = [
        pltpu.make_async_copy(grad_hbm, gext.at[0, pl.ds(1, ROWS)], lsem.at[1]),
        pltpu.make_async_copy(act_hbm, act.at[0], lsem.at[0]),
        pltpu.make_async_copy(gather_hbm.at[core], gather, lsem.at[2]),
        pltpu.make_async_copy(permt_hbm, permt, lsem.at[3]),
        pltpu.make_async_copy(spread_hbm, spr, lsem.at[4]),
        pltpu.make_async_copy(piece_ref.at[0], wp.at[0, zh, x, zl, y], lsem.at[5]),
        pltpu.make_async_copy(piece_ref.at[1], wp.at[1, zh, x, zl, y], lsem.at[6]),
    ]
    for c in local:
        c.start()
    s2r[...] = jnp.zeros_like(s2r)
    t2r[...] = jnp.zeros_like(t2r)

    sent = []

    def remote(src, dst, ss, rs, dev):
        c = pltpu.make_async_remote_copy(
            src_ref=src, dst_ref=dst, send_sem=ss, recv_sem=rs, device_id=dev, device_id_type=MESH
        )
        c.start()
        sent.append(c)
        return c

    def received(copies):
        for c in copies:
            c.wait_recv()

    pl.semaphore_wait(barrier, len(partners))
    halo = [
        remote(grad_hbm.at[ROWS - 1], gext.at[0, 0], hsem.at[0], hrec.at[0], down),
        remote(grad_hbm.at[0], gext.at[0, ROWS + 1], hsem.at[1], hrec.at[1], up),
    ]
    here = (zh, x, zl, y)
    gx = [
        remote(piece_ref.at[1], wp.at[(1, *here)], gsem.at[i], grec.at[i], xdev[i])
        for i in range(3)
    ]
    gy = [
        remote(piece_ref.at[0], wp.at[(0, *here)], gsem.at[3 + i], grec.at[3 + i], ydev[i])
        for i in range(7)
    ]
    swap = [
        remote(grad_hbm, gext.at[1, pl.ds(1, ROWS)], psem.at[0], prec.at[0], pair),
        remote(act_hbm, act.at[1], psem.at[1], prec.at[1], pair),
    ]

    lane = lax.broadcasted_iota(jnp.int32, (80, WIDTH), 1)
    zero8 = jnp.zeros((8, WIDTH), F32)

    def fill(img, e, keep=None):
        col = pl.ds(pl.multiple_of((img * 8 + e) * WIDTH, WIDTH), WIDTH)
        for pr in range(4):
            g = gext[img, e, 80 * pr : 80 * pr + 80, :].astype(F32)
            if keep is not None:
                g = jnp.where(keep, g, 0.0)
            nxt = jnp.where(lane == WIDTH - 1, 0.0, pltpu.roll(g, WIDTH - 1, 1))
            prv = jnp.where(lane == 0, 0.0, pltpu.roll(g, 1, 1))
            for h in range(2):
                sl = slice(40 * h, 40 * h + 40)
                block = jnp.concatenate([nxt[sl], g[sl], prv[sl], zero8], axis=0)
                base = (2 * pr + h) * 128
                q[base : base + 128, col] = block.astype(BF16)

    def fill_image(img):
        @pl.loop(1, ROWS + 1)
        def _(e):
            fill(img, e)

    def rows_image(img):
        for h in range(0, ROWS, 2):
            both = jnp.concatenate([act[img, h], act[img, h + 1]], axis=1)
            base = img * ROWS * WIDTH + h * WIDTH
            amat[:, base : base + 2 * WIDTH] = fdot(gather[...], both).astype(BF16)

    local[0].wait()
    fill_image(0)
    local[1].wait()
    local[2].wait()
    rows_image(0)

    received(gx)
    local[6].wait()
    gz1 = [
        remote(wp.at[1, zh, :, zl, y], wp.at[1, zh, :, zl, y], gsem.at[10 + i], grec.at[10 + i], zdev[i])
        for i in range(7)
    ]
    received(gy)
    local[5].wait()
    gz0 = [
        remote(wp.at[0, zh, x, zl], wp.at[0, zh, x, zl], gsem.at[17 + i], grec.at[17 + i], zdev[i])
        for i in range(7)
    ]

    swap[0].wait_recv()
    fill_image(1)
    received(halo)
    forward = [
        remote(gext.at[0, e], gext.at[1, e], fsem.at[i], frec.at[i], pair)
        for i, e in enumerate((0, ROWS + 1))
    ]
    swap[1].wait_recv()
    rows_image(1)

    span = ROWS * WIDTH

    def partial(j):
        rows_a = slice(0, HALF) if j < 2 else slice(HALF, 352)

        @pl.loop(0, 4)
        def _(n):
            rows = pl.ds(pl.multiple_of(n * 256, 256), 256)
            total = fdot(amat[rows_a, 0:span], q[rows, (2 - j) * WIDTH : (2 - j) * WIDTH + span], NT)
            total = total + fdot(
                amat[rows_a, span : 2 * span], q[rows, (10 - j) * WIDTH : (10 - j) * WIDTH + span], NT
            )
            for h in range(2):
                sidx = 2 * n + h
                one = total[:, 128 * h : 128 * h + 128]
                if j < 2:
                    p[j, sidx // NX, lax.rem(sidx, NX)] = one.reshape(ZL, 40, 128)
                else:
                    p2[sidx // NX, lax.rem(sidx, NX)] = one.reshape(NY, 24, 128)

    partial(1)
    x1 = [
        remote(p.at[1, :, xs[i]], rx1.at[i], xsem.at[i], xrec.at[i], xdev[i]) for i in range(NX - 1)
    ]

    received(gz1)
    gy1 = [
        remote(wp.at[1, :, :, :, y], wp.at[1, :, :, :, y], gsem.at[24 + i], grec.at[24 + i], ydev[i])
        for i in range(7)
    ]
    received(gz0)
    gx0 = [
        remote(wp.at[0, :, x], wp.at[0, :, x], gsem.at[31 + i], grec.at[31 + i], xdev[i])
        for i in range(3)
    ]

    top, bottom = strip > 0, strip < 7
    fill(0, 0, top)
    fill(0, ROWS + 1, bottom)
    forward[0].wait_recv()
    fill(1, 0, top)
    forward[1].wait_recv()
    fill(1, ROWS + 1, bottom)

    flows = ((1, 0, 4), (-1, 0, 3), (1, 1, 3), (-1, 1, 4))

    def ring(me, own, slots, ss, rs, devs):
        def send(f, k, src):
            sign = flows[f][0]
            return remote(src, slots.at[f, k], ss.at[f, k], rs.at[f, k], devs[0 if sign > 0 else 6])

        hops = {}

        def start():
            for f, (sign, part, steps) in enumerate(flows):
                dest = lax.rem(me + 8 + sign * steps, 8)
                hops[f, 0] = send(f, 0, own(dest, part))

        def step(k):
            for f, (sign, part, steps) in enumerate(flows):
                if k < steps:
                    hops[f, k - 1].wait_recv()
                    dest = lax.rem(me + 8 + sign * (steps - k), 8)
                    slots[f, k - 1] = slots[f, k - 1] + own(dest, part)[...]
                    hops[f, k] = send(f, k, slots.at[f, k - 1])

        def finish(part):
            total = own(me, part)[...]
            for f, (sign, fpart, steps) in enumerate(flows):
                if fpart == part:
                    hops[f, steps - 1].wait_recv()
                    total = total + slots[f, steps - 1]
            return total

        return start, step, finish

    def own_z(dest, part):
        return p.at[0, dest // ZL, pl.ds(2 * part, 2), lax.rem(dest, ZL)]

    def own_y(dest, part):
        return p2.at[part, :, dest]

    zstart, zstep, zfinish = ring(z, own_z, rz1, zsem, zrec, zdev)
    ystart, ystep, yfinish = ring(y, own_y, ry1, rsem, rrec, ydev)

    partial(0)
    zstart()
    partial(2)
    ystart()
    for k in range(1, 4):
        zstep(k)
        ystep(k)

    received(x1)
    for h in range(2):
        total = p[1, h, x]
        for i in range(NX - 1):
            total = total + rx1[i, h]
        s1a[h] = total
    z2 = [
        remote(s1a.at[zs[i] // ZL, lax.rem(zs[i], ZL)], rz2.at[i], z2sem.at[i], z2rec.at[i], zdev[i])
        for i in range(NZ - 1)
    ]
    for part in range(2):
        s1b[2 * part : 2 * part + 2] = zfinish(part)
    x2 = [
        remote(s1b.at[xs[i]], rx2.at[i], x2sem.at[i], x2rec.at[i], xdev[i]) for i in range(NX - 1)
    ]
    for part in range(2):
        s1c[part] = yfinish(part)
    x3 = [
        remote(s1c.at[:, xs[i]], rx3.at[i], x3sem.at[i], x3rec.at[i], xdev[i]) for i in range(NX - 1)
    ]

    received(gx0)
    received(gy1)
    local[4].wait()
    for pr in range(4):
        cols = []
        for sidx in (2 * pr, 2 * pr + 1):
            halves = [
                wp[half, sidx // NX, sidx % NX].astype(F32).reshape(32, 8, 128) for half in range(2)
            ]
            cols.append(jnp.concatenate(halves, axis=1).reshape(512, 128).astype(BF16))
        both = jnp.concatenate(cols, axis=1)
        wmat[:, 256 * pr : 256 * pr + 256] = fdot(spr[...], both).astype(BF16)

    def image(img, put):
        for h in range(0, ROWS, 2):
            total = None
            for j in range(3):
                base = (img * 8 + h + 2 - j) * WIDTH
                term = fdot(wmat[HALF * j : HALF * j + HALF, :], q[:, base : base + 256])
                total = term if total is None else total + term
            total = total.astype(BF16)
            put(h, total[:, :WIDTH])
            put(h + 1, total[:, WIDTH:])

    mine = pl.ds(pl.multiple_of(core * HALF, HALF), HALF)

    def put_peer(h, v):
        igs[h] = v

    def put_own(h, v):
        igr[h, mine, :] = v

    image(1, put_peer)
    back = remote(igs, igr.at[:, mine], isem, irec, pair)

    received(x2)
    total = s1b[x]
    for i in range(NX - 1):
        total = total + rx2[i]
    s2[0] = total
    received(x3)
    total = s1c[:, x]
    for i in range(NX - 1):
        total = total + rx3[i]
    t2[...] = total
    for h in range(2):
        for v in range(ZL):
            t2r[h, v, 0:KI, :] = t2[h, KI * v : KI * v + KI, :]
    z3 = [
        remote(t2r.at[zs[i] // ZL, lax.rem(zs[i], ZL)], rz3.at[i], z3sem.at[i], z3rec.at[i], zdev[i])
        for i in range(NZ - 1)
    ]
    received(z2)
    total = s1a[zh, zl]
    for i in range(NZ - 1):
        total = total + rz2[i]
    s2[1] = total
    for j in range(2):
        for v in range(NY):
            s2r[v, j, 0:KI, :] = s2[j, KI * v : KI * v + KI, :]
    y3 = [
        remote(s2r.at[ys[i]], ry.at[i], ysem.at[i], yrec.at[i], ydev[i]) for i in range(NY - 1)
    ]

    image(0, put_own)
    local[3].wait()
    back.wait_recv()
    for h in range(0, ROWS, 2):
        both = jnp.concatenate([igr[h], igr[h + 1]], axis=1)
        out = fdot(permt[...], both).astype(BF16)
        ig_ref[h] = out[:, :WIDTH]
        ig_ref[h + 1] = out[:, WIDTH:]

    received(z3)
    total = t2r[zh, zl]
    for i in range(NZ - 1):
        total = total + rz3[i]
    kg_ref[2] = total * scale
    received(y3)
    total = s2r[y]
    for i in range(NY - 1):
        total = total + ry[i]
    kg_ref[0:2] = total * scale
    for c in sent:
        c.wait_send()


def body(activations, out_grad, weights):
    cells = 64 * 48 * 128
    scale = 1.0 / math.sqrt(cells)
    act = jnp.transpose(activations[0], (1, 0, 2))
    grad = jnp.transpose(out_grad[0], (1, 0, 2))
    piece = jnp.transpose(weights.reshape(KI, 3, 3, KO), (1, 0, 2, 3)).reshape(3 * KI, 3 * KO)
    piece = jnp.pad(piece, ((0, 1), (0, 8))).reshape(2, 8, 128)
    gather, perm = permutation()
    hbm = pl.BlockSpec(memory_space=pltpu.HBM)
    vmem = pl.BlockSpec(memory_space=pltpu.VMEM)
    V = pltpu.VMEM
    D = pltpu.SemaphoreType.DMA

    def run(*args):
        kernel(scale, *args)

    ig, kg = pl.pallas_call(
        run,
        out_shape=(
            jax.ShapeDtypeStruct((ROWS, CH, WIDTH), BF16),
            jax.ShapeDtypeStruct((3, 8, 128), F32),
        ),
        in_specs=[hbm, hbm, vmem, hbm, hbm, hbm],
        out_specs=(vmem, vmem),
        scratch_shapes=[
            V((2, ROWS, CH, WIDTH), BF16),
            V((2, 8, CH, WIDTH), BF16),
            V((352, CH), BF16),
            V((CH, CH), BF16),
            V((3 * HALF, 512), BF16),
            V((352, 2 * ROWS * WIDTH), BF16),
            V((1024, 2048), BF16),
            V((2, 2, NX, ZL, 40, 128), F32),
            V((2, NX, NY, 24, 128), F32),
            V((2, 2, NX, ZL, NY, 8, 128), BF16),
            V((3 * HALF, 1024), BF16),
            V((ROWS, HALF, WIDTH), BF16),
            V((ROWS, CH, WIDTH), BF16),
            V((NX - 1, 2, ZL, 40, 128), F32),
            V((4, 4, 2, 40, 128), F32),
            V((4, 4, NX, 24, 128), F32),
            V((2, ZL, 40, 128), F32),
            V((NX, 40, 128), F32),
            V((2, NX, 24, 128), F32),
            V((NX - 1, 40, 128), F32),
            V((NX - 1, 2, 24, 128), F32),
            V((NZ - 1, 40, 128), F32),
            V((2, 40, 128), F32),
            V((NY, 2, 8, 128), F32),
            V((NY - 1, 2, 8, 128), F32),
            V((2, 24, 128), F32),
            V((2, ZL, 8, 128), F32),
            V((NZ - 1, 8, 128), F32),
            D((7,)), D((2,)), D((2,)), D((2,)), D((2,)), D((2,)), D((2,)), D((34,)), D((34,)),
            D((3,)), D((3,)), D((4, 4)), D((4, 4)), D((4, 4)), D((4, 4)),
            D((3,)), D((3,)), D((3,)), D((3,)), D((7,)), D((7,)), D((7,)), D((7,)), D((7,)), D((7,)),
            D(()), D(()),
        ],
        compiler_params=pltpu.CompilerParams(
            collective_id=0, has_side_effects=True, vmem_limit_bytes=60 << 20
        ),
    )(
        act, grad, piece,
        jnp.asarray(gather, BF16), jnp.asarray(perm, BF16), jnp.asarray(spread(), BF16),
    )
    input_grad = jnp.transpose(ig, (1, 0, 2))[None]
    kg = kg[:, :KI, : 3 * KO].reshape(3, KI, 3, KO)
    kernel_grad = jnp.transpose(kg, (1, 0, 2, 3)).reshape(KI, 9, KO)
    return input_grad, kernel_grad


def solution(mesh):
    in_specs = (
        P("band", None, "strip", None),
        P("band", None, "strip", None),
        P("band", None, "strip"),
    )
    out_specs = (P("band", None, "strip", None), P("band", None, "strip"))
    return jax.shard_map(body, mesh=mesh, in_specs=in_specs, out_specs=out_specs, check_vma=False)
```

time: 66.3 us -> 67.9 us (1.024)
  the two profiles are of different devices: /device:TPU:1 before, /device:TPU:2 now
where the time goes in v2:
time: 67.9 us; the launch traced here: 67.6 us
  Pallas kernels  62.3 us (92%)
  local copies, waits for them, and re-layouts  4.69 us (7%)
    pallas_call x1, Pallas kernels, body(): pl.pallas_call(run, out_shape=(jax.ShapeDtypeStruct((ROWS, CH, WIDTH), BF...  62.3 us
    unnamed x1, local copies, waits for them, and re-layouts  1.84 us

profile of v2, /device:TPU:2, one launch (start us, length us, event | category | flops | bytes accessed | tf_op | source)
XLA Modules:
  0.0 67.6 jit_solution(3412404670397732149)
XLA Ops:
  0.6 0.7 %copy.13 = bf16[3,5,3,40]{3,2,1,0:T(4,128)(2,1)S(1)} copy(bf16[3,5,3,40]{3,1,2,0:T(8,128)(2,1)} %bitcast.24) | data formatting | bytes 7200 | tf_op jit(solution)/shard_map/transpose | solution.py:397
  1.4 0.1 reshape.20
  1.5 0.6 pad_bitcast_fusion.args_2_
  2.1 62.3 %shard_map.77 = (bf16[6,320,128]{2,1,0:T(8,128)(2,1)}, f32[3,8,128]{2,1,0:T(8,128)}) custom-call(bf16[6,320,128]{2,1,0:T(8,128)(2,1)} %bitcast.19, bf16[6,320,128]{2,1,0:T(8,128)(2,1)} %bitcast.20, bf16[2,8,128]{2,1,0:T(8,128)(2,1)} %pad_bitcast_fusion.args_2_, bf16[2,352,320]{2,1,0:T(8,128)(2,1)} %constant.9.clone.args_3_, ...), custom_call_target="tpu_custom_call" | custom-call | tf_op jit(solution)/shard_map/pallas_call | solution.py:408
  64.3 0.7 %copy.14 = f32[3,5,120]{2,0,1:T(4,128)S(1)} copy(f32[3,5,120]{2,1,0:T(8,128)} %bitcast.25) | data formatting | bytes 14400 | tf_op jit(solution)/shard_map/slice | solution.py:458
  65.1 0.1 reshape.22
  65.1 0.6 copy.15
  65.8 1.8 %copy.17 = bf16[1,320,6,128]{3,1,2,0:T(8,128)(2,1)} copy(bf16[1,320,6,128]{3,1,2,0:T(8,128)(2,1)} %bitcast.21) | data formatting | bytes 983040

commit v3 on v2

v3 whole, which is shorter than its diff:
```python
import math

import jax
import jax.numpy as jnp
import numpy as np
from jax import lax
from jax.experimental import pallas as pl
from jax.experimental.pallas import tpu as pltpu
from jax.sharding import PartitionSpec as P

MESH = pl.DeviceIdType.MESH
BF16 = jnp.bfloat16
F32 = jnp.float32

ROWS = 6
CH = 320
WIDTH = 128
NX, NY, NZ = 4, 8, 8
ZL = 4
KI = 5
KO = 40
HALF = CH // 2
NT = (((1,), (1,)), ((), ()))


def row_order():
    rows = {0: [], 1: [], 2: []}
    for y in range(NY):
        for k in range(4):
            rows[1] += [(zl, y, k) for zl in range(ZL)]
    for zl in range(ZL):
        rows[1] += [(zl, y, 4) for y in range(NY)]
    for ks in ((0, 1), (2, 3, 4)):
        for zl in range(ZL):
            for k in ks:
                rows[0] += [(zl, y, k) for y in range(NY)]
    for zl in range(ZL):
        for k in (0, 1, 2):
            rows[2] += [(zl, y, k) for y in range(NY)]
    for y in range(NY):
        for k in (3, 4):
            rows[2] += [(zl, y, k) for zl in range(ZL)]
    return rows[0] + rows[1] + rows[2]


def permutation():
    perm = np.zeros((CH, CH), np.float32)
    gather = np.zeros((2, 3 * HALF, CH), np.float32)
    for core in range(2):
        for m in range(HALF):
            perm[2 * KI * (m // KI) + KI * core + m % KI, core * HALF + m] = 1.0
        for m, (zl, y, k) in enumerate(row_order()):
            gather[core, m, 2 * KI * (zl * NY + y) + KI * core + k] = 1.0
    return gather, perm


def spread():
    out = np.zeros((3 * HALF, 32 * 16), np.float32)
    for j in range(3):
        for m in range(HALF):
            out[j * HALF + m, 16 * (m // KI) + j * KI + m % KI] = 1.0
    return out


def fdot(a, b, dims=(((1,), (0,)), ((), ()))):
    return lax.dot_general(a, b, dims, preferred_element_type=F32)


def kernel(
    scale, act_hbm, grad_hbm, piece_ref, gather_hbm, permt_hbm, spread_hbm,
    ig_ref, kg_ref,
    act, gext, gather, permt, spr, amat, q, wp, wmat, igs, igr,
    pxe, pxl, pze, pzl, py, rxe, rxl, rze, rzl, ry1,
    sxe, sxl, sz, sy, ry2, rz2, rx2, rx3, ty, tyr, ry3, tz, tzr, rz3,
    lsem, psem, prec, hsem, hrec, fsem, frec, gsem, grec, xsem, xrec, zsem, zrec, y1sem, y1rec,
    y2sem, y2rec, z2sem, z2rec, x2sem, x2rec, x3sem, x3rec, y3sem, y3rec, z3sem, z3rec, isem, irec,
):
    band = lax.axis_index("band")
    strip = lax.axis_index("strip")
    core = lax.rem(band, 2)
    y = lax.rem(band // 2, NY)
    zl = band // (2 * NY)
    x = lax.rem(strip, NX)
    zh = strip // NX
    z = zh * ZL + zl

    def at(zz, yy, xx):
        zzh, zzl = zz // ZL, lax.rem(zz, ZL)
        return ((zzl * NY + yy) * 2 + core, zzh * NX + xx)

    pair = (band + 1 - 2 * core, strip)
    down = (band, lax.rem(strip + 1, 8))
    up = (band, lax.rem(strip + 7, 8))
    xs = [lax.rem(x + d, NX) for d in range(1, NX)]
    ys = [lax.rem(y + d, NY) for d in range(1, NY)]
    zs = [lax.rem(z + d, NZ) for d in range(1, NZ)]
    xdev = [at(z, y, v) for v in xs]
    ydev = [at(z, v, x) for v in ys]
    zdev = [at(v, y, x) for v in zs]

    barrier = pltpu.get_barrier_semaphore()
    partners = [pair, down, up] + xdev + ydev + zdev
    for dev in partners:
        pl.semaphore_signal(barrier, inc=1, device_id=dev, device_id_type=MESH)

    local = [
        pltpu.make_async_copy(grad_hbm, gext.at[0, pl.ds(1, ROWS)], lsem.at[1]),
        pltpu.make_async_copy(act_hbm, act.at[0], lsem.at[0]),
        pltpu.make_async_copy(gather_hbm.at[core], gather, lsem.at[2]),
        pltpu.make_async_copy(permt_hbm, permt, lsem.at[3]),
        pltpu.make_async_copy(spread_hbm, spr, lsem.at[4]),
        pltpu.make_async_copy(piece_ref.at[0], wp.at[0, zh, x, zl, y], lsem.at[5]),
        pltpu.make_async_copy(piece_ref.at[1], wp.at[1, zh, x, zl, y], lsem.at[6]),
    ]
    for c in local:
        c.start()
    tyr[...] = jnp.zeros_like(tyr)
    tzr[...] = jnp.zeros_like(tzr)
    kg_ref[...] = jnp.zeros_like(kg_ref)

    sent = []

    def remote(src, dst, ss, rs, dev):
        c = pltpu.make_async_remote_copy(
            src_ref=src, dst_ref=dst, send_sem=ss, recv_sem=rs, device_id=dev, device_id_type=MESH
        )
        c.start()
        sent.append(c)
        return c

    def received(copies):
        for c in copies:
            c.wait_recv()

    pl.semaphore_wait(barrier, len(partners))
    inner, outer = strip > 0, strip < 7
    halo_down = []
    halo_up = []
    for n in range(4):
        part = pl.ds(80 * n, 80)
        halo_down.append(
            pltpu.make_async_remote_copy(
                src_ref=grad_hbm.at[ROWS - 1, part], dst_ref=gext.at[0, 0, part],
                send_sem=hsem.at[0, n], recv_sem=hrec.at[0, n], device_id=down, device_id_type=MESH,
            )
        )
        halo_up.append(
            pltpu.make_async_remote_copy(
                src_ref=grad_hbm.at[0, part], dst_ref=gext.at[0, ROWS + 1, part],
                send_sem=hsem.at[1, n], recv_sem=hrec.at[1, n], device_id=up, device_id_type=MESH,
            )
        )

    @pl.when(outer)
    def _():
        for c in halo_down:
            c.start()

    @pl.when(inner)
    def _():
        for c in halo_up:
            c.start()

    here = (zh, x, zl, y)
    gx = [
        remote(piece_ref.at[1], wp.at[(1, *here)], gsem.at[i], grec.at[i], xdev[i])
        for i in range(3)
    ]
    gy = [
        remote(piece_ref.at[0], wp.at[(0, *here)], gsem.at[3 + i], grec.at[3 + i], ydev[i])
        for i in range(7)
    ]
    swap = [
        remote(grad_hbm, gext.at[1, pl.ds(1, ROWS)], psem.at[0], prec.at[0], pair),
        remote(act_hbm, act.at[1], psem.at[1], prec.at[1], pair),
    ]

    lane = lax.broadcasted_iota(jnp.int32, (80, WIDTH), 1)
    zero8 = jnp.zeros((8, WIDTH), F32)

    def fill(img, e, keep=None, parts=range(4)):
        col = pl.ds(pl.multiple_of((img * 8 + e) * WIDTH, WIDTH), WIDTH)
        for pr in parts:
            g = gext[img, e, 80 * pr : 80 * pr + 80, :].astype(F32)
            if keep is not None:
                g = jnp.where(keep, g, 0.0)
            nxt = jnp.where(lane == WIDTH - 1, 0.0, pltpu.roll(g, WIDTH - 1, 1))
            prv = jnp.where(lane == 0, 0.0, pltpu.roll(g, 1, 1))
            for h in range(2):
                sl = slice(40 * h, 40 * h + 40)
                block = jnp.concatenate([nxt[sl], g[sl], prv[sl], zero8], axis=0)
                base = (2 * pr + h) * 128
                q[base : base + 128, col] = block.astype(BF16)

    def fill_image(img):
        @pl.loop(1, ROWS + 1)
        def _(e):
            fill(img, e)

    def rows_image(img):
        for h in range(0, ROWS, 2):
            both = jnp.concatenate([act[img, h], act[img, h + 1]], axis=1)
            base = img * ROWS * WIDTH + h * WIDTH
            amat[:, base : base + 2 * WIDTH] = fdot(gather[...], both).astype(BF16)

    def forward(n):
        part = pl.ds(80 * n, 80)

        @pl.when(inner)
        def _():
            halo_down[n].wait_recv()

        @pl.when(outer)
        def _():
            halo_up[n].wait_recv()

        return [
            remote(gext.at[0, e, part], gext.at[1, e, part], fsem.at[i, n], frec.at[i, n], pair)
            for i, e in enumerate((0, ROWS + 1))
        ]

    local[0].wait()
    fill_image(0)
    received(gx)
    local[6].wait()
    gz1 = [
        remote(wp.at[1, zh, :, zl, y], wp.at[1, zh, :, zl, y], gsem.at[10 + i], grec.at[10 + i], zdev[i])
        for i in range(7)
    ]
    received(gy)
    local[5].wait()
    gz0 = [
        remote(wp.at[0, zh, x, zl], wp.at[0, zh, x, zl], gsem.at[17 + i], grec.at[17 + i], zdev[i])
        for i in range(7)
    ]
    local[1].wait()
    local[2].wait()
    rows_image(0)
    swap[0].wait_recv()
    fill_image(1)
    swap[1].wait_recv()
    rows_image(1)
    received(gz0)
    gx0 = [
        remote(wp.at[0, :, x], wp.at[0, :, x], gsem.at[31 + i], grec.at[31 + i], xdev[i])
        for i in range(3)
    ]
    received(gz1)
    gy1 = [
        remote(wp.at[1, :, :, :, y], wp.at[1, :, :, :, y], gsem.at[24 + i], grec.at[24 + i], ydev[i])
        for i in range(7)
    ]

    span = ROWS * WIDTH

    def product(j, n):
        rows = pl.ds(256 * n if isinstance(n, int) else pl.multiple_of(n * 256, 256), 256)
        mine = slice(HALF * j, HALF * j + HALF)
        total = fdot(amat[mine, 0:span], q[rows, (2 - j) * WIDTH : (2 - j) * WIDTH + span], NT)
        return total + fdot(
            amat[mine, span : 2 * span], q[rows, (10 - j) * WIDTH : (10 - j) * WIDTH + span], NT
        )

    @pl.loop(0, 4)
    def _(n):
        total = product(1, n)
        for h in range(2):
            sh, sx = n // 2, 2 * lax.rem(n, 2) + h
            one = total[:, 128 * h : 128 * h + 128]
            pxe[sh, sx] = one[:128].reshape(NY, 16, 128)
            pze[sh, sx] = one[128:].reshape(ZL, 8, 128)

    xe = [
        remote(pxe.at[:, xs[i]], rxe.at[i], xsem.at[0, i], xrec.at[0, i], xdev[i]) for i in range(3)
    ]
    ze = [
        remote(
            pze.at[zs[i] // ZL, :, lax.rem(zs[i], ZL)], rze.at[i], zsem.at[0, i], zrec.at[0, i], zdev[i]
        )
        for i in range(7)
    ]

    ahead = forward(0)
    for n in range(4):
        now = ahead
        if n < 3:
            ahead = forward(n + 1)
        fill(0, 0, inner, (n,))
        fill(0, ROWS + 1, outer, (n,))
        now[0].wait_recv()
        fill(1, 0, inner, (n,))
        now[1].wait_recv()
        fill(1, ROWS + 1, outer, (n,))
        first = product(0, n)
        third = product(2, n)
        for h in range(2):
            sh, sx = n // 2, 2 * (n % 2) + h
            one = first[:, 128 * h : 128 * h + 128]
            pxl[sh, sx, :, 0:16] = one[:64].reshape(ZL, 16, 128)
            pzl[sh, sx] = one[64:].reshape(ZL, 24, 128)
            one = third[:, 128 * h : 128 * h + 128]
            pxl[sh, sx, :, 16:40] = one[:96].reshape(ZL, 24, 128)
            py[sh, sx] = one[96:].reshape(NY, 8, 128)

    zlate = [
        remote(
            pzl.at[zs[i] // ZL, :, lax.rem(zs[i], ZL)], rzl.at[i], zsem.at[1, i], zrec.at[1, i], zdev[i]
        )
        for i in range(7)
    ]
    y1 = [remote(py.at[:, :, ys[i]], ry1.at[i], y1sem.at[i], y1rec.at[i], ydev[i]) for i in range(7)]
    xl = [
        remote(pxl.at[:, xs[i]], rxl.at[i], xsem.at[1, i], xrec.at[1, i], xdev[i]) for i in range(3)
    ]

    received(gx0)
    received(gy1)
    local[4].wait()
    for pr in range(4):
        cols = []
        for sidx in (2 * pr, 2 * pr + 1):
            halves = [
                wp[half, sidx // NX, sidx % NX].astype(F32).reshape(32, 8, 128) for half in range(2)
            ]
            cols.append(jnp.concatenate(halves, axis=1).reshape(512, 128).astype(BF16))
        both = jnp.concatenate(cols, axis=1)
        wmat[:, 256 * pr : 256 * pr + 256] = fdot(spr[...], both).astype(BF16)

    def image(img, put):
        for h in range(0, ROWS, 2):
            total = None
            for j in range(3):
                base = (img * 8 + h + 2 - j) * WIDTH
                term = fdot(wmat[HALF * j : HALF * j + HALF, :], q[:, base : base + 256])
                total = term if total is None else total + term
            total = total.astype(BF16)
            put(h, total[:, :WIDTH])
            put(h + 1, total[:, WIDTH:])

    mine = pl.ds(pl.multiple_of(core * HALF, HALF), HALF)

    def put_peer(h, v):
        igs[h] = v

    def put_own(h, v):
        igr[h, mine, :] = v

    image(1, put_peer)
    back = remote(igs, igr.at[:, mine], isem, irec, pair)

    image(0, put_own)

    received(xe)
    for h in range(2):
        total = pxe[h, x]
        for i in range(3):
            total = total + rxe[i, h]
        sxe[h] = total
    y2 = [remote(sxe.at[:, ys[i]], ry2.at[i], y2sem.at[i], y2rec.at[i], ydev[i]) for i in range(7)]
    received(y1)
    total = py[:, :, y]
    for i in range(7):
        total = total + ry1[i]
    sy[...] = total
    x3 = [remote(sy.at[:, xs[i]], rx3.at[i], x3sem.at[i], x3rec.at[i], xdev[i]) for i in range(3)]
    received(xl)
    for h in range(2):
        total = pxl[h, x]
        for i in range(3):
            total = total + rxl[i, h]
        sxl[h] = total
    z2 = [
        remote(sxl.at[zs[i] // ZL, lax.rem(zs[i], ZL)], rz2.at[i], z2sem.at[i], z2rec.at[i], zdev[i])
        for i in range(7)
    ]
    received(ze)
    received(zlate)
    early = pze[zh, :, zl]
    late = pzl[zh, :, zl]
    for i in range(7):
        early = early + rze[i]
        late = late + rzl[i]
    sz[:, 0:8] = early
    sz[:, 8:32] = late
    x2 = [remote(sz.at[xs[i]], rx2.at[i], x2sem.at[i], x2rec.at[i], xdev[i]) for i in range(3)]

    received(y2)
    total = sxe[:, y]
    for i in range(7):
        total = total + ry2[i]
    tz[:, 0:16] = total
    received(x3)
    total = sy[:, x]
    for i in range(3):
        total = total + rx3[i]
    tz[:, 16:24] = total
    for h in range(2):
        for v in range(ZL):
            for k in range(6):
                tzr[h, v, k : k + 1, :] = tz[h, ZL * k + v : ZL * k + v + 1, :]
    z3 = [
        remote(tzr.at[zs[i] // ZL, lax.rem(zs[i], ZL)], rz3.at[i], z3sem.at[i], z3rec.at[i], zdev[i])
        for i in range(7)
    ]
    received(z2)
    total = sxl[zh, zl]
    for i in range(7):
        total = total + rz2[i]
    ty[0:40] = total
    received(x2)
    total = sz[x]
    for i in range(3):
        total = total + rx2[i]
    ty[40:72] = total
    for v in range(NY):
        for k in range(9):
            tyr[v, k : k + 1, :] = ty[NY * k + v : NY * k + v + 1, :]
    y3 = [remote(tyr.at[ys[i]], ry3.at[i], y3sem.at[i], y3rec.at[i], ydev[i]) for i in range(7)]

    local[3].wait()
    back.wait_recv()
    for h in range(0, ROWS, 2):
        both = jnp.concatenate([igr[h], igr[h + 1]], axis=1)
        out = fdot(permt[...], both).astype(BF16)
        ig_ref[h] = out[:, :WIDTH]
        ig_ref[h + 1] = out[:, WIDTH:]

    received(z3)
    total = tzr[zh, zl]
    for i in range(7):
        total = total + rz3[i]
    total = total * scale
    kg_ref[1, 0:4] = total[0:4]
    kg_ref[2, 3:5] = total[4:6]
    received(y3)
    total = tyr[y]
    for i in range(7):
        total = total + ry3[i]
    total = total * scale
    kg_ref[0, 0:2] = total[0:2]
    kg_ref[2, 0:3] = total[2:5]
    kg_ref[1, 4:5] = total[5:6]
    kg_ref[0, 2:5] = total[6:9]
    for c in sent:
        c.wait_send()

    @pl.when(outer)
    def _():
        for c in halo_down:
            c.wait_send()

    @pl.when(inner)
    def _():
        for c in halo_up:
            c.wait_send()


def body(activations, out_grad, weights):
    cells = 64 * 48 * 128
    scale = 1.0 / math.sqrt(cells)
    act = jnp.transpose(activations[0], (1, 0, 2))
    grad = jnp.transpose(out_grad[0], (1, 0, 2))
    piece = jnp.transpose(weights.reshape(KI, 3, 3, KO), (1, 0, 2, 3)).reshape(3 * KI, 3 * KO)
    piece = jnp.pad(piece, ((0, 1), (0, 8))).reshape(2, 8, 128)
    gather, perm = permutation()
    hbm = pl.BlockSpec(memory_space=pltpu.HBM)
    vmem = pl.BlockSpec(memory_space=pltpu.VMEM)
    V = pltpu.VMEM
    D = pltpu.SemaphoreType.DMA

    def run(*args):
        kernel(scale, *args)

    ig, kg = pl.pallas_call(
        run,
        out_shape=(
            jax.ShapeDtypeStruct((ROWS, CH, WIDTH), BF16),
            jax.ShapeDtypeStruct((3, 8, 128), F32),
        ),
        in_specs=[hbm, hbm, vmem, hbm, hbm, hbm],
        out_specs=(vmem, vmem),
        scratch_shapes=[
            V((2, ROWS, CH, WIDTH), BF16),
            V((2, 8, CH, WIDTH), BF16),
            V((3 * HALF, CH), BF16),
            V((CH, CH), BF16),
            V((3 * HALF, 512), BF16),
            V((3 * HALF, 2 * ROWS * WIDTH), BF16),
            V((1024, 2048), BF16),
            V((2, 2, NX, ZL, NY, 8, 128), BF16),
            V((3 * HALF, 1024), BF16),
            V((ROWS, HALF, WIDTH), BF16),
            V((ROWS, CH, WIDTH), BF16),
            V((2, NX, NY, 16, 128), F32),
            V((2, NX, ZL, 40, 128), F32),
            V((2, NX, ZL, 8, 128), F32),
            V((2, NX, ZL, 24, 128), F32),
            V((2, NX, NY, 8, 128), F32),
            V((3, 2, NY, 16, 128), F32),
            V((3, 2, ZL, 40, 128), F32),
            V((7, NX, 8, 128), F32),
            V((7, NX, 24, 128), F32),
            V((7, 2, NX, 8, 128), F32),
            V((2, NY, 16, 128), F32),
            V((2, ZL, 40, 128), F32),
            V((NX, 32, 128), F32),
            V((2, NX, 8, 128), F32),
            V((7, 2, 16, 128), F32),
            V((7, 40, 128), F32),
            V((3, 32, 128), F32),
            V((3, 2, 8, 128), F32),
            V((72, 128), F32),
            V((NY, 16, 128), F32),
            V((7, 16, 128), F32),
            V((2, 24, 128), F32),
            V((2, ZL, 8, 128), F32),
            V((7, 8, 128), F32),
            D((7,)), D((2,)), D((2,)), D((2, 4)), D((2, 4)), D((2, 4)), D((2, 4)), D((34,)), D((34,)),
            D((2, 3)), D((2, 3)), D((2, 7)), D((2, 7)), D((7,)), D((7,)), D((7,)), D((7,)), D((7,)), D((7,)),
            D((3,)), D((3,)), D((3,)), D((3,)), D((7,)), D((7,)), D((7,)), D((7,)), D(()), D(()),
        ],
        compiler_params=pltpu.CompilerParams(
            collective_id=0, has_side_effects=True, vmem_limit_bytes=60 << 20
        ),
    )(
        act, grad, piece,
        jnp.asarray(gather, BF16), jnp.asarray(perm, BF16), jnp.asarray(spread(), BF16),
    )
    input_grad = jnp.transpose(ig, (1, 0, 2))[None]
    kg = kg[:, :KI, : 3 * KO].reshape(3, KI, 3, KO)
    kernel_grad = jnp.transpose(kg, (1, 0, 2, 3)).reshape(KI, 9, KO)
    return input_grad, kernel_grad


def solution(mesh):
    in_specs = (
        P("band", None, "strip", None),
        P("band", None, "strip", None),
        P("band", None, "strip"),
    )
    out_specs = (P("band", None, "strip", None), P("band", None, "strip"))
    return jax.shard_map(body, mesh=mesh, in_specs=in_specs, out_specs=out_specs, check_vma=False)
```

time: 67.9 us -> 65.7 us (0.968)
  the two profiles are of different devices: /device:TPU:2 before, /device:TPU:4 now
where the time goes in v3:
time: 65.7 us; the launch traced here: 65.4 us
  Pallas kernels  60.1 us (91%)
  local copies, waits for them, and re-layouts  4.69 us (7%)
    pallas_call x1, Pallas kernels, body(): pl.pallas_call(run, out_shape=(jax.ShapeDtypeStruct((ROWS, CH, WIDTH), BF...  60.1 us
    unnamed x1, local copies, waits for them, and re-layouts  1.84 us

profile of v3, /device:TPU:4, one launch (start us, length us, event | category | flops | bytes accessed | tf_op | source)
XLA Modules:
  0.0 65.4 jit_solution(4358557438716246602)
XLA Ops:
  0.6 0.7 %copy.13 = bf16[3,5,3,40]{3,2,1,0:T(4,128)(2,1)S(1)} copy(bf16[3,5,3,40]{3,1,2,0:T(8,128)(2,1)} %bitcast.24) | data formatting | bytes 7200 | tf_op jit(solution)/shard_map/transpose | solution.py:463
  1.4 0.1 reshape.20
  1.5 0.6 pad_bitcast_fusion.args_2_
  2.1 60.1 %shard_map.77 = (bf16[6,320,128]{2,1,0:T(8,128)(2,1)}, f32[3,8,128]{2,1,0:T(8,128)}) custom-call(bf16[6,320,128]{2,1,0:T(8,128)(2,1)} %bitcast.19, bf16[6,320,128]{2,1,0:T(8,128)(2,1)} %bitcast.20, bf16[2,8,128]{2,1,0:T(8,128)(2,1)} %pad_bitcast_fusion.args_2_, bf16[2,480,320]{2,1,0:T(8,128)(2,1)} %constant.9.clone.args_3_, ...), custom_call_target="tpu_custom_call" | custom-call | tf_op jit(solution)/shard_map/pallas_call | solution.py:474
  62.2 0.7 %copy.14 = f32[3,5,120]{2,0,1:T(4,128)S(1)} copy(f32[3,5,120]{2,1,0:T(8,128)} %bitcast.25) | data formatting | bytes 14400 | tf_op jit(solution)/shard_map/slice | solution.py:530
  62.9 0.1 reshape.22
  63.0 0.6 copy.15
  63.6 1.8 %copy.17 = bf16[1,320,6,128]{3,1,2,0:T(8,128)(2,1)} copy(bf16[1,320,6,128]{3,1,2,0:T(8,128)(2,1)} %bitcast.21) | data formatting | bytes 983040

commit v4 on v3

--- a/solution.py
+++ b/solution.py
@@ -221,18 +221,6 @@
 
     local[0].wait()
     fill_image(0)
-    received(gx)
-    local[6].wait()
-    gz1 = [
-        remote(wp.at[1, zh, :, zl, y], wp.at[1, zh, :, zl, y], gsem.at[10 + i], grec.at[10 + i], zdev[i])
-        for i in range(7)
-    ]
-    received(gy)
-    local[5].wait()
-    gz0 = [
-        remote(wp.at[0, zh, x, zl], wp.at[0, zh, x, zl], gsem.at[17 + i], grec.at[17 + i], zdev[i])
-        for i in range(7)
-    ]
     local[1].wait()
     local[2].wait()
     rows_image(0)
@@ -240,17 +228,6 @@
     fill_image(1)
     swap[1].wait_recv()
     rows_image(1)
-    received(gz0)
-    gx0 = [
-        remote(wp.at[0, :, x], wp.at[0, :, x], gsem.at[31 + i], grec.at[31 + i], xdev[i])
-        for i in range(3)
-    ]
-    received(gz1)
-    gy1 = [
-        remote(wp.at[1, :, :, :, y], wp.at[1, :, :, :, y], gsem.at[24 + i], grec.at[24 + i], ydev[i])
-        for i in range(7)
-    ]
-
     span = ROWS * WIDTH
 
     def product(j, n):
@@ -280,6 +257,18 @@
         for i in range(7)
     ]
 
+    received(gx)
+    local[6].wait()
+    gz1 = [
+        remote(wp.at[1, zh, :, zl, y], wp.at[1, zh, :, zl, y], gsem.at[10 + i], grec.at[10 + i], zdev[i])
+        for i in range(7)
+    ]
+    received(gy)
+    local[5].wait()
+    gz0 = [
+        remote(wp.at[0, zh, x, zl], wp.at[0, zh, x, zl], gsem.at[17 + i], grec.at[17 + i], zdev[i])
+        for i in range(7)
+    ]
     ahead = forward(0)
     for n in range(4):
         now = ahead
@@ -313,43 +302,16 @@
         remote(pxl.at[:, xs[i]], rxl.at[i], xsem.at[1, i], xrec.at[1, i], xdev[i]) for i in range(3)
     ]
 
-    received(gx0)
-    received(gy1)
-    local[4].wait()
-    for pr in range(4):
-        cols = []
-        for sidx in (2 * pr, 2 * pr + 1):
-            halves = [
-                wp[half, sidx // NX, sidx % NX].astype(F32).reshape(32, 8, 128) for half in range(2)
-            ]
-            cols.append(jnp.concatenate(halves, axis=1).reshape(512, 128).astype(BF16))
-        both = jnp.concatenate(cols, axis=1)
-        wmat[:, 256 * pr : 256 * pr + 256] = fdot(spr[...], both).astype(BF16)
-
-    def image(img, put):
-        for h in range(0, ROWS, 2):
-            total = None
-            for j in range(3):
-                base = (img * 8 + h + 2 - j) * WIDTH
-                term = fdot(wmat[HALF * j : HALF * j + HALF, :], q[:, base : base + 256])
-                total = term if total is None else total + term
-            total = total.astype(BF16)
-            put(h, total[:, :WIDTH])
-            put(h + 1, total[:, WIDTH:])
-
-    mine = pl.ds(pl.multiple_of(core * HALF, HALF), HALF)
-
-    def put_peer(h, v):
-        igs[h] = v
-
-    def put_own(h, v):
-        igr[h, mine, :] = v
-
-    image(1, put_peer)
-    back = remote(igs, igr.at[:, mine], isem, irec, pair)
-
-    image(0, put_own)
-
+    received(gz0)
+    gx0 = [
+        remote(wp.at[0, :, x], wp.at[0, :, x], gsem.at[31 + i], grec.at[31 + i], xdev[i])
+        for i in range(3)
+    ]
+    received(gz1)
+    gy1 = [
+        remote(wp.at[1, :, :, :, y], wp.at[1, :, :, :, y], gsem.at[24 + i], grec.at[24 + i], ydev[i])
+        for i in range(7)
+    ]
     received(xe)
     for h in range(2):
         total = pxe[h, x]
@@ -384,6 +346,41 @@
     sz[:, 8:32] = late
     x2 = [remote(sz.at[xs[i]], rx2.at[i], x2sem.at[i], x2rec.at[i], xdev[i]) for i in range(3)]
 
+    received(gx0)
+    received(gy1)
+    local[4].wait()
+    for pr in range(4):
+        cols = []
+        for sidx in (2 * pr, 2 * pr + 1):
+            halves = [
+                wp[half, sidx // NX, sidx % NX].astype(F32).reshape(32, 8, 128) for half in range(2)
+            ]
+            cols.append(jnp.concatenate(halves, axis=1).reshape(512, 128).astype(BF16))
+        both = jnp.concatenate(cols, axis=1)
+        wmat[:, 256 * pr : 256 * pr + 256] = fdot(spr[...], both).astype(BF16)
+
+    def image(img, put):
+        for h in range(0, ROWS, 2):
+            total = None
+            for j in range(3):
+                base = (img * 8 + h + 2 - j) * WIDTH
+                term = fdot(wmat[HALF * j : HALF * j + HALF, :], q[:, base : base + 256])
+                total = term if total is None else total + term
+            total = total.astype(BF16)
+            put(h, total[:, :WIDTH])
+            put(h + 1, total[:, WIDTH:])
+
+    mine = pl.ds(pl.multiple_of(core * HALF, HALF), HALF)
+
+    def put_peer(h, v):
+        igs[h] = v
+
+    def put_own(h, v):
+        igr[h, mine, :] = v
+
+    image(1, put_peer)
+    back = remote(igs, igr.at[:, mine], isem, irec, pair)
+
     received(y2)
     total = sxe[:, y]
     for i in range(7):
@@ -417,6 +414,7 @@
             tyr[v, k : k + 1, :] = ty[NY * k + v : NY * k + v + 1, :]
     y3 = [remote(tyr.at[ys[i]], ry3.at[i], y3sem.at[i], y3rec.at[i], ydev[i]) for i in range(7)]
 
+    image(0, put_own)
     local[3].wait()
     back.wait_recv()
     for h in range(0, ROWS, 2):

time: 65.7 us -> 62.2 us (0.947)
  the two profiles are of different devices: /device:TPU:4 before, /device:TPU:1 now
where the time goes in v4:
time: 62.2 us; the launch traced here: 61.7 us
  Pallas kernels  56.4 us (91%)
  local copies, waits for them, and re-layouts  4.69 us (8%)
  between operations  0.64 us (1%)
    pallas_call x1, Pallas kernels, body(): pl.pallas_call(run, out_shape=(jax.ShapeDtypeStruct((ROWS, CH, WIDTH), BF...  56.4 us
    unnamed x1, local copies, waits for them, and re-layouts  1.84 us

profile of v4, /device:TPU:1, one launch (start us, length us, event | category | flops | bytes accessed | tf_op | source)
XLA Modules:
  0.0 61.7 jit_solution(16455914502547639154)
XLA Ops:
  0.6 0.7 %copy.13 = bf16[3,5,3,40]{3,2,1,0:T(4,128)(2,1)S(1)} copy(bf16[3,5,3,40]{3,1,2,0:T(8,128)(2,1)} %bitcast.24) | data formatting | bytes 7200 | tf_op jit(solution)/shard_map/transpose | solution.py:461
  1.4 0.1 reshape.20
  1.5 0.6 pad_bitcast_fusion.args_2_
  2.1 56.4 %shard_map.77 = (bf16[6,320,128]{2,1,0:T(8,128)(2,1)}, f32[3,8,128]{2,1,0:T(8,128)}) custom-call(bf16[6,320,128]{2,1,0:T(8,128)(2,1)} %bitcast.19, bf16[6,320,128]{2,1,0:T(8,128)(2,1)} %bitcast.20, bf16[2,8,128]{2,1,0:T(8,128)(2,1)} %pad_bitcast_fusion.args_2_, bf16[2,480,320]{2,1,0:T(8,128)(2,1)} %constant.9.clone.args_3_, ...), custom_call_target="tpu_custom_call" | custom-call | tf_op jit(solution)/shard_map/pallas_call | solution.py:472
  58.5 0.7 %copy.14 = f32[3,5,120]{2,0,1:T(4,128)S(1)} copy(f32[3,5,120]{2,1,0:T(8,128)} %bitcast.25) | data formatting | bytes 14400 | tf_op jit(solution)/shard_map/slice | solution.py:528
  59.2 0.1 reshape.22
  59.3 0.6 %copy.15 = f32[5,3,3,40]{3,0,2,1:T(8,128)} copy(f32[5,3,3,40]{3,2,1,0:T(4,128)S(1)} %bitcast.22) | data formatting | bytes 14400 | tf_op jit(solution)/shard_map/transpose | solution.py:529
  59.9 1.8 %copy.17 = bf16[1,320,6,128]{3,1,2,0:T(8,128)(2,1)} copy(bf16[1,320,6,128]{3,1,2,0:T(8,128)(2,1)} %bitcast.21) | data formatting | bytes 983040

commit v5 on v4

--- a/solution.py
+++ b/solution.py
@@ -67,9 +67,9 @@
 
 
 def kernel(
-    scale, act_hbm, grad_hbm, piece_ref, gather_hbm, permt_hbm, spread_hbm,
+    scale, act_hbm, grad_hbm, taps_ref, gather_hbm, permt_hbm, spread_hbm,
     ig_ref, kg_ref,
-    act, gext, gather, permt, spr, amat, q, wp, wmat, igs, igr,
+    piece_ref, act, gext, gather, permt, spr, amat, q, wp, wmat, igs, igr,
     pxe, pxl, pze, pzl, py, rxe, rxl, rze, rzl, ry1,
     sxe, sxl, sz, sy, ry2, rz2, rx2, rx3, ty, tyr, ry3, tz, tzr, rz3,
     lsem, psem, prec, hsem, hrec, fsem, frec, gsem, grec, xsem, xrec, zsem, zrec, y1sem, y1rec,
@@ -109,14 +109,18 @@
         pltpu.make_async_copy(gather_hbm.at[core], gather, lsem.at[2]),
         pltpu.make_async_copy(permt_hbm, permt, lsem.at[3]),
         pltpu.make_async_copy(spread_hbm, spr, lsem.at[4]),
-        pltpu.make_async_copy(piece_ref.at[0], wp.at[0, zh, x, zl, y], lsem.at[5]),
-        pltpu.make_async_copy(piece_ref.at[1], wp.at[1, zh, x, zl, y], lsem.at[6]),
     ]
     for c in local:
         c.start()
+    rows = []
+    for j in range(3):
+        cols = [taps_ref[3 * j + c].astype(F32) for c in range(3)]
+        rows.append(jnp.concatenate(cols + [jnp.zeros((KI, 8), F32)], axis=1))
+    block = jnp.concatenate(rows + [jnp.zeros((1, 128), F32)], axis=0).reshape(2, 8, 128)
+    piece_ref[...] = block.astype(BF16)
+    wp[:, zh, x, zl, y] = block.astype(BF16)
     tyr[...] = jnp.zeros_like(tyr)
     tzr[...] = jnp.zeros_like(tzr)
-    kg_ref[...] = jnp.zeros_like(kg_ref)
 
     sent = []
 
@@ -168,7 +172,7 @@
     ]
     gy = [
         remote(piece_ref.at[0], wp.at[(0, *here)], gsem.at[3 + i], grec.at[3 + i], ydev[i])
-        for i in range(7)
+        for i in (3, 2, 4, 1, 5, 0, 6)
     ]
     swap = [
         remote(grad_hbm, gext.at[1, pl.ds(1, ROWS)], psem.at[0], prec.at[0], pair),
@@ -254,20 +258,18 @@
         remote(
             pze.at[zs[i] // ZL, :, lax.rem(zs[i], ZL)], rze.at[i], zsem.at[0, i], zrec.at[0, i], zdev[i]
         )
-        for i in range(7)
+        for i in (3, 2, 4, 1, 5, 0, 6)
     ]
 
     received(gx)
-    local[6].wait()
     gz1 = [
         remote(wp.at[1, zh, :, zl, y], wp.at[1, zh, :, zl, y], gsem.at[10 + i], grec.at[10 + i], zdev[i])
-        for i in range(7)
+        for i in (3, 2, 4, 1, 5, 0, 6)
     ]
     received(gy)
-    local[5].wait()
     gz0 = [
         remote(wp.at[0, zh, x, zl], wp.at[0, zh, x, zl], gsem.at[17 + i], grec.at[17 + i], zdev[i])
-        for i in range(7)
+        for i in (3, 2, 4, 1, 5, 0, 6)
     ]
     ahead = forward(0)
     for n in range(4):
@@ -295,9 +297,9 @@
         remote(
             pzl.at[zs[i] // ZL, :, lax.rem(zs[i], ZL)], rzl.at[i], zsem.at[1, i], zrec.at[1, i], zdev[i]
         )
-        for i in range(7)
-    ]
-    y1 = [remote(py.at[:, :, ys[i]], ry1.at[i], y1sem.at[i], y1rec.at[i], ydev[i]) for i in range(7)]
+        for i in (3, 2, 4, 1, 5, 0, 6)
+    ]
+    y1 = [remote(py.at[:, :, ys[i]], ry1.at[i], y1sem.at[i], y1rec.at[i], ydev[i]) for i in (3, 2, 4, 1, 5, 0, 6)]
     xl = [
         remote(pxl.at[:, xs[i]], rxl.at[i], xsem.at[1, i], xrec.at[1, i], xdev[i]) for i in range(3)
     ]
@@ -310,7 +312,7 @@
     received(gz1)
     gy1 = [
         remote(wp.at[1, :, :, :, y], wp.at[1, :, :, :, y], gsem.at[24 + i], grec.at[24 + i], ydev[i])
-        for i in range(7)
+        for i in (3, 2, 4, 1, 5, 0, 6)
     ]
     received(xe)
     for h in range(2):
@@ -318,7 +320,7 @@
         for i in range(3):
             total = total + rxe[i, h]
         sxe[h] = total
-    y2 = [remote(sxe.at[:, ys[i]], ry2.at[i], y2sem.at[i], y2rec.at[i], ydev[i]) for i in range(7)]
+    y2 = [remote(sxe.at[:, ys[i]], ry2.at[i], y2sem.at[i], y2rec.at[i], ydev[i]) for i in (3, 2, 4, 1, 5, 0, 6)]
     received(y1)
     total = py[:, :, y]
     for i in range(7):
@@ -333,7 +335,7 @@
         sxl[h] = total
     z2 = [
         remote(sxl.at[zs[i] // ZL, lax.rem(zs[i], ZL)], rz2.at[i], z2sem.at[i], z2rec.at[i], zdev[i])
-        for i in range(7)
+        for i in (3, 2, 4, 1, 5, 0, 6)
     ]
     received(ze)
     received(zlate)
@@ -397,7 +399,7 @@
                 tzr[h, v, k : k + 1, :] = tz[h, ZL * k + v : ZL * k + v + 1, :]
     z3 = [
         remote(tzr.at[zs[i] // ZL, lax.rem(zs[i], ZL)], rz3.at[i], z3sem.at[i], z3rec.at[i], zdev[i])
-        for i in range(7)
+        for i in (3, 2, 4, 1, 5, 0, 6)
     ]
     received(z2)
     total = sxl[zh, zl]
@@ -412,7 +414,7 @@
     for v in range(NY):
         for k in range(9):
             tyr[v, k : k + 1, :] = ty[NY * k + v : NY * k + v + 1, :]
-    y3 = [remote(tyr.at[ys[i]], ry3.at[i], y3sem.at[i], y3rec.at[i], ydev[i]) for i in range(7)]
+    y3 = [remote(tyr.at[ys[i]], ry3.at[i], y3sem.at[i], y3rec.at[i], ydev[i]) for i in (3, 2, 4, 1, 5, 0, 6)]
 
     image(0, put_own)
     local[3].wait()
@@ -428,17 +430,22 @@
     for i in range(7):
         total = total + rz3[i]
     total = total * scale
-    kg_ref[1, 0:4] = total[0:4]
-    kg_ref[2, 3:5] = total[4:6]
+
+    def put(j, k0, rows):
+        for c in range(3):
+            kg_ref[3 * j + c, k0 : k0 + rows.shape[0], :] = rows[:, 40 * c : 40 * c + 40]
+
+    put(1, 0, total[0:4])
+    put(2, 3, total[4:6])
     received(y3)
     total = tyr[y]
     for i in range(7):
         total = total + ry3[i]
     total = total * scale
-    kg_ref[0, 0:2] = total[0:2]
-    kg_ref[2, 0:3] = total[2:5]
-    kg_ref[1, 4:5] = total[5:6]
-    kg_ref[0, 2:5] = total[6:9]
+    put(0, 0, total[0:2])
+    put(2, 0, total[2:5])
+    put(1, 4, total[5:6])
+    put(0, 2, total[6:9])
     for c in sent:
         c.wait_send()
 
@@ -458,8 +465,7 @@
     scale = 1.0 / math.sqrt(cells)
     act = jnp.transpose(activations[0], (1, 0, 2))
     grad = jnp.transpose(out_grad[0], (1, 0, 2))
-    piece = jnp.transpose(weights.reshape(KI, 3, 3, KO), (1, 0, 2, 3)).reshape(3 * KI, 3 * KO)
-    piece = jnp.pad(piece, ((0, 1), (0, 8))).reshape(2, 8, 128)
+    piece = jnp.transpose(weights, (1, 0, 2))
     gather, perm = permutation()
     hbm = pl.BlockSpec(memory_space=pltpu.HBM)
     vmem = pl.BlockSpec(memory_space=pltpu.VMEM)
@@ -473,11 +479,12 @@
         run,
         out_shape=(
             jax.ShapeDtypeStruct((ROWS, CH, WIDTH), BF16),
-            jax.ShapeDtypeStruct((3, 8, 128), F32),
+            jax.ShapeDtypeStruct((9, KI, KO), F32),
         ),
         in_specs=[hbm, hbm, vmem, hbm, hbm, hbm],
         out_specs=(vmem, vmem),
         scratch_shapes=[
+            V((2, 8, 128), BF16),
             V((2, ROWS, CH, WIDTH), BF16),
             V((2, 8, CH, WIDTH), BF16),
             V((3 * HALF, CH), BF16),
@@ -513,7 +520,7 @@
             V((2, 24, 128), F32),
             V((2, ZL, 8, 128), F32),
             V((7, 8, 128), F32),
-            D((7,)), D((2,)), D((2,)), D((2, 4)), D((2, 4)), D((2, 4)), D((2, 4)), D((34,)), D((34,)),
+            D((5,)), D((2,)), D((2,)), D((2, 4)), D((2, 4)), D((2, 4)), D((2, 4)), D((34,)), D((34,)),
             D((2, 3)), D((2, 3)), D((2, 7)), D((2, 7)), D((7,)), D((7,)), D((7,)), D((7,)), D((7,)), D((7,)),
             D((3,)), D((3,)), D((3,)), D((3,)), D((7,)), D((7,)), D((7,)), D((7,)), D(()), D(()),
         ],
@@ -525,8 +532,7 @@
         jnp.asarray(gather, BF16), jnp.asarray(perm, BF16), jnp.asarray(spread(), BF16),
     )
     input_grad = jnp.transpose(ig, (1, 0, 2))[None]
-    kg = kg[:, :KI, : 3 * KO].reshape(3, KI, 3, KO)
-    kernel_grad = jnp.transpose(kg, (1, 0, 2, 3)).reshape(KI, 9, KO)
+    kernel_grad = jnp.transpose(kg, (1, 0, 2))
     return input_grad, kernel_grad
 
 

time: 62.2 us -> 59.3 us (0.953)
  local copies, waits for them, and re-layouts: 4.69 us -> 2.47 us
    transpose x2 -> x0, local copies, waits for them, and re-layouts: 1.36 us -> none  [the longest x1 0.73 us: body(): jnp.transpose(weights.reshape(KI, 3, 3, KO), (1, 0, 2, 3))]
    reshape x3 -> x0, local copies, waits for them, and re-layouts: 0.78 us -> none  [the longest x1 0.6 us: body(): piece = jnp.pad(piece, ((0, 1), (0, 8))).reshape(2, 8, 128)]
    slice x1 -> x0, local copies, waits for them, and re-layouts: 0.71 us -> none  [body(): kg = kg[:, :KI, :3 * KO].reshape(3, KI, 3, KO)]
    pallas_call x1, Pallas kernels: 56.4 us -> 55.8 us  [body(): pl.pallas_call(run, out_shape=(jax.ShapeDtypeStruct((ROWS, CH, WIDTH), BF...]
    unnamed x1 -> x4, local copies, waits for them, and re-layouts: 1.84 us -> 2.47 us
where the time goes in v5:
time: 59.3 us; the launch traced here: 58.9 us
  Pallas kernels  55.8 us (94%)
  local copies, waits for them, and re-layouts  2.47 us (4%)
  between operations  0.65 us (1%)
    pallas_call x1, Pallas kernels, body(): pl.pallas_call(run, out_shape=(jax.ShapeDtypeStruct((ROWS, CH, WIDTH), BF...  55.8 us
    unnamed x4, local copies, waits for them, and re-layouts  2.47 us

profile of v5, /device:TPU:1, one launch (start us, length us, event | category | flops | bytes accessed | tf_op | source)
XLA Modules:
  0.0 58.9 jit_solution(14777608696345762478)
XLA Ops:
  0.6 55.8 %shard_map.77 = (bf16[6,320,128]{2,1,0:T(8,128)(2,1)}, f32[9,5,40]{2,1,0:T(8,128)}) custom-call(bf16[6,320,128]{2,1,0:T(8,128)(2,1)} %bitcast.11, bf16[6,320,128]{2,1,0:T(8,128)(2,1)} %bitcast.12, bf16[9,5,40]{2,1,0:T(8,128)(2,1)} %bitcast.15, bf16[2,480,320]{2,1,0:T(8,128)(2,1)} %constant.6.clone.args_3_, bf16[320,320]{1,0:T(8,128)(2,1)} %constant.7.clone.args_4_, ...), custom_call_target="tpu_custom_call" | custom-call | tf_op jit(solution)/shard_map/pallas_call | solution.py:478
  56.4 0.0 copy-start
  56.4 1.8 %copy.10 = bf16[1,320,6,128]{3,1,2,0:T(8,128)(2,1)} copy(bf16[1,320,6,128]{3,1,2,0:T(8,128)(2,1)} %bitcast.13) | data formatting | bytes 983040
  58.3 0.0 copy-done
  58.3 0.6 %copy.11 = f32[5,9,40]{2,0,1:T(8,128)} copy(f32[5,9,40]{2,0,1:T(8,128)S(1)} %bitcast.14) | data formatting | bytes 14400
Async XLA Ops:
  56.4 1.9 %copy-start = (f32[9,5,40]{2,1,0:T(8,128)S(1)}, f32[9,5,40]{2,1,0:T(8,128)}, u32[]{:S(2)}) copy-start(f32[9,5,40]{2,1,0:T(8,128)} %get-tuple-element.5) | copy-start | bytes 21604

commit v6 on v5

--- a/solution.py
+++ b/solution.py
@@ -304,15 +304,15 @@
         remote(pxl.at[:, xs[i]], rxl.at[i], xsem.at[1, i], xrec.at[1, i], xdev[i]) for i in range(3)
     ]
 
+    received(gz1)
+    gy1 = [
+        remote(wp.at[1, :, :, :, y], wp.at[1, :, :, :, y], gsem.at[24 + i], grec.at[24 + i], ydev[i])
+        for i in (3, 2, 4, 1, 5, 0, 6)
+    ]
     received(gz0)
     gx0 = [
         remote(wp.at[0, :, x], wp.at[0, :, x], gsem.at[31 + i], grec.at[31 + i], xdev[i])
         for i in range(3)
-    ]
-    received(gz1)
-    gy1 = [
-        remote(wp.at[1, :, :, :, y], wp.at[1, :, :, :, y], gsem.at[24 + i], grec.at[24 + i], ydev[i])
-        for i in (3, 2, 4, 1, 5, 0, 6)
     ]
     received(xe)
     for h in range(2):
@@ -348,41 +348,6 @@
     sz[:, 8:32] = late
     x2 = [remote(sz.at[xs[i]], rx2.at[i], x2sem.at[i], x2rec.at[i], xdev[i]) for i in range(3)]
 
-    received(gx0)
-    received(gy1)
-    local[4].wait()
-    for pr in range(4):
-        cols = []
-        for sidx in (2 * pr, 2 * pr + 1):
-            halves = [
-                wp[half, sidx // NX, sidx % NX].astype(F32).reshape(32, 8, 128) for half in range(2)
-            ]
-            cols.append(jnp.concatenate(halves, axis=1).reshape(512, 128).astype(BF16))
-        both = jnp.concatenate(cols, axis=1)
-        wmat[:, 256 * pr : 256 * pr + 256] = fdot(spr[...], both).astype(BF16)
-
-    def image(img, put):
-        for h in range(0, ROWS, 2):
-            total = None
-            for j in range(3):
-                base = (img * 8 + h + 2 - j) * WIDTH
-                term = fdot(wmat[HALF * j : HALF * j + HALF, :], q[:, base : base + 256])
-                total = term if total is None else total + term
-            total = total.astype(BF16)
-            put(h, total[:, :WIDTH])
-            put(h + 1, total[:, WIDTH:])
-
-    mine = pl.ds(pl.multiple_of(core * HALF, HALF), HALF)
-
-    def put_peer(h, v):
-        igs[h] = v
-
-    def put_own(h, v):
-        igr[h, mine, :] = v
-
-    image(1, put_peer)
-    back = remote(igs, igr.at[:, mine], isem, irec, pair)
-
     received(y2)
     total = sxe[:, y]
     for i in range(7):
@@ -415,6 +380,41 @@
         for k in range(9):
             tyr[v, k : k + 1, :] = ty[NY * k + v : NY * k + v + 1, :]
     y3 = [remote(tyr.at[ys[i]], ry3.at[i], y3sem.at[i], y3rec.at[i], ydev[i]) for i in (3, 2, 4, 1, 5, 0, 6)]
+
+    received(gx0)
+    received(gy1)
+    local[4].wait()
+    for pr in range(4):
+        cols = []
+        for sidx in (2 * pr, 2 * pr + 1):
+            halves = [
+                wp[half, sidx // NX, sidx % NX].astype(F32).reshape(32, 8, 128) for half in range(2)
+            ]
+            cols.append(jnp.concatenate(halves, axis=1).reshape(512, 128).astype(BF16))
+        both = jnp.concatenate(cols, axis=1)
+        wmat[:, 256 * pr : 256 * pr + 256] = fdot(spr[...], both).astype(BF16)
+
+    def image(img, put):
+        for h in range(0, ROWS, 2):
+            total = None
+            for j in range(3):
+                base = (img * 8 + h + 2 - j) * WIDTH
+                term = fdot(wmat[HALF * j : HALF * j + HALF, :], q[:, base : base + 256])
+                total = term if total is None else total + term
+            total = total.astype(BF16)
+            put(h, total[:, :WIDTH])
+            put(h + 1, total[:, WIDTH:])
+
+    mine = pl.ds(pl.multiple_of(core * HALF, HALF), HALF)
+
+    def put_peer(h, v):
+        igs[h] = v
+
+    def put_own(h, v):
+        igr[h, mine, :] = v
+
+    image(1, put_peer)
+    back = remote(igs, igr.at[:, mine], isem, irec, pair)
 
     image(0, put_own)
     local[3].wait()

time: 59.3 us -> 59 us (level)
  no operation moved by 1% of the time
where the time goes in v6:
time: 59 us; the launch traced here: 58.6 us
  Pallas kernels  55.5 us (94%)
  local copies, waits for them, and re-layouts  2.47 us (4%)
  between operations  0.65 us (1%)
    pallas_call x1, Pallas kernels, body(): pl.pallas_call(run, out_shape=(jax.ShapeDtypeStruct((ROWS, CH, WIDTH), BF...  55.5 us
    unnamed x4, local copies, waits for them, and re-layouts  2.47 us

profile of v6, /device:TPU:1, one launch (start us, length us, event | category | flops | bytes accessed | tf_op | source)
XLA Modules:
  0.0 58.6 jit_solution(2243067333052342909)
XLA Ops:
  0.6 55.5 %shard_map.77 = (bf16[6,320,128]{2,1,0:T(8,128)(2,1)}, f32[9,5,40]{2,1,0:T(8,128)}) custom-call(bf16[6,320,128]{2,1,0:T(8,128)(2,1)} %bitcast.11, bf16[6,320,128]{2,1,0:T(8,128)(2,1)} %bitcast.12, bf16[9,5,40]{2,1,0:T(8,128)(2,1)} %bitcast.15, bf16[2,480,320]{2,1,0:T(8,128)(2,1)} %constant.6.clone.args_3_, bf16[320,320]{1,0:T(8,128)(2,1)} %constant.7.clone.args_4_, ...), custom_call_target="tpu_custom_call" | custom-call | tf_op jit(solution)/shard_map/pallas_call | solution.py:478
  56.1 0.0 copy-start
  56.1 1.8 %copy.10 = bf16[1,320,6,128]{3,1,2,0:T(8,128)(2,1)} copy(bf16[1,320,6,128]{3,1,2,0:T(8,128)(2,1)} %bitcast.13) | data formatting | bytes 983040
  57.9 0.0 copy-done
  57.9 0.6 %copy.11 = f32[5,9,40]{2,0,1:T(8,128)} copy(f32[5,9,40]{2,0,1:T(8,128)S(1)} %bitcast.14) | data formatting | bytes 14400
Async XLA Ops:
  56.1 1.9 %copy-start = (f32[9,5,40]{2,1,0:T(8,128)S(1)}, f32[9,5,40]{2,1,0:T(8,128)}, u32[]{:S(2)}) copy-start(f32[9,5,40]{2,1,0:T(8,128)} %get-tuple-element.5) | copy-start | bytes 21604

commit v7 on v6

--- a/solution.py
+++ b/solution.py
@@ -168,7 +168,7 @@
     here = (zh, x, zl, y)
     gx = [
         remote(piece_ref.at[1], wp.at[(1, *here)], gsem.at[i], grec.at[i], xdev[i])
-        for i in range(3)
+        for i in (1, 0, 2)
     ]
     gy = [
         remote(piece_ref.at[0], wp.at[(0, *here)], gsem.at[3 + i], grec.at[3 + i], ydev[i])
@@ -252,7 +252,7 @@
             pze[sh, sx] = one[128:].reshape(ZL, 8, 128)
 
     xe = [
-        remote(pxe.at[:, xs[i]], rxe.at[i], xsem.at[0, i], xrec.at[0, i], xdev[i]) for i in range(3)
+        remote(pxe.at[:, xs[i]], rxe.at[i], xsem.at[0, i], xrec.at[0, i], xdev[i]) for i in (1, 0, 2)
     ]
     ze = [
         remote(
@@ -301,7 +301,7 @@
     ]
     y1 = [remote(py.at[:, :, ys[i]], ry1.at[i], y1sem.at[i], y1rec.at[i], ydev[i]) for i in (3, 2, 4, 1, 5, 0, 6)]
     xl = [
-        remote(pxl.at[:, xs[i]], rxl.at[i], xsem.at[1, i], xrec.at[1, i], xdev[i]) for i in range(3)
+        remote(pxl.at[:, xs[i]], rxl.at[i], xsem.at[1, i], xrec.at[1, i], xdev[i]) for i in (1, 0, 2)
     ]
 
     received(gz1)
@@ -312,7 +312,7 @@
     received(gz0)
     gx0 = [
         remote(wp.at[0, :, x], wp.at[0, :, x], gsem.at[31 + i], grec.at[31 + i], xdev[i])
-        for i in range(3)
+        for i in (1, 0, 2)
     ]
     received(xe)
     for h in range(2):
@@ -326,7 +326,7 @@
     for i in range(7):
         total = total + ry1[i]
     sy[...] = total
-    x3 = [remote(sy.at[:, xs[i]], rx3.at[i], x3sem.at[i], x3rec.at[i], xdev[i]) for i in range(3)]
+    x3 = [remote(sy.at[:, xs[i]], rx3.at[i], x3sem.at[i], x3rec.at[i], xdev[i]) for i in (1, 0, 2)]
     received(xl)
     for h in range(2):
         total = pxl[h, x]
@@ -346,7 +346,7 @@
         late = late + rzl[i]
     sz[:, 0:8] = early
     sz[:, 8:32] = late
-    x2 = [remote(sz.at[xs[i]], rx2.at[i], x2sem.at[i], x2rec.at[i], xdev[i]) for i in range(3)]
+    x2 = [remote(sz.at[xs[i]], rx2.at[i], x2sem.at[i], x2rec.at[i], xdev[i]) for i in (1, 0, 2)]
 
     received(y2)
     total = sxe[:, y]

time: 59 us -> 59.7 us (1.012)
  Pallas kernels: 55.5 us -> 56.4 us
    pallas_call x1, Pallas kernels: 55.5 us -> 56.4 us  [body(): pl.pallas_call(run, out_shape=(jax.ShapeDtypeStruct((ROWS, CH, WIDTH), BF...]
where the time goes in v7:
time: 59.7 us; the launch traced here: 59.5 us
  Pallas kernels  56.4 us (94%)
  local copies, waits for them, and re-layouts  2.47 us (4%)
  between operations  0.65 us (1%)
    pallas_call x1, Pallas kernels, body(): pl.pallas_call(run, out_shape=(jax.ShapeDtypeStruct((ROWS, CH, WIDTH), BF...  56.4 us
    unnamed x4, local copies, waits for them, and re-layouts  2.47 us

profile of v7, /device:TPU:1, one launch (start us, length us, event | category | flops | bytes accessed | tf_op | source)
XLA Modules:
  0.0 59.5 jit_solution(14969836211771778831)
XLA Ops:
  0.6 56.4 %shard_map.77 = (bf16[6,320,128]{2,1,0:T(8,128)(2,1)}, f32[9,5,40]{2,1,0:T(8,128)}) custom-call(bf16[6,320,128]{2,1,0:T(8,128)(2,1)} %bitcast.11, bf16[6,320,128]{2,1,0:T(8,128)(2,1)} %bitcast.12, bf16[9,5,40]{2,1,0:T(8,128)(2,1)} %bitcast.15, bf16[2,480,320]{2,1,0:T(8,128)(2,1)} %constant.6.clone.args_3_, bf16[320,320]{1,0:T(8,128)(2,1)} %constant.7.clone.args_4_, ...), custom_call_target="tpu_custom_call" | custom-call | tf_op jit(solution)/shard_map/pallas_call | solution.py:478
  57.0 0.0 copy-start
  57.0 1.8 %copy.10 = bf16[1,320,6,128]{3,1,2,0:T(8,128)(2,1)} copy(bf16[1,320,6,128]{3,1,2,0:T(8,128)(2,1)} %bitcast.13) | data formatting | bytes 983040
  58.9 0.0 copy-done
  58.9 0.6 %copy.11 = f32[5,9,40]{2,0,1:T(8,128)} copy(f32[5,9,40]{2,0,1:T(8,128)S(1)} %bitcast.14) | data formatting | bytes 14400
Async XLA Ops:
  57.0 1.9 %copy-start = (f32[9,5,40]{2,1,0:T(8,128)S(1)}, f32[9,5,40]{2,1,0:T(8,128)}, u32[]{:S(2)}) copy-start(f32[9,5,40]{2,1,0:T(8,128)} %get-tuple-element.5) | copy-start | bytes 21604
